TPU v7x, 128 devices: a whole 4x4x4 slice. The times are simulated.
128 devices in a mesh: dp: 16 (over x, z), blk: 8 (over y, core).
Axes of the slice: x: 4, y: 4, z: 4, core: 2. Of those that a mesh axis runs over, the one named last changes fastest.
Arguments:
- entity_table: float32 [262144, 400], P(('dp', 'blk')), may hold values from -1.8 to 1.8
- adagrad_sum: float32 [262144], P(('dp', 'blk')), may hold values from 0.0001 to 0.001
- relations: float32 [7424, 400], replicated, may hold values from -1.8 to 1.8
- owner_map: int32 [262144], replicated, may hold values from 0 to 262143, as said below
- head_ids: int32 [16384], P(('dp', 'blk')), may hold values from 0 to 262143, as said below
- rel_ids: int32 [16384], P(('dp', 'blk')), may hold values from 0 to 7423
- tail_ids: int32 [16384], P(('dp', 'blk')), may hold values from 0 to 262143, as said below
- neg_ids: int32 [65536], P(('dp', 'blk')), may hold values from 0 to 262143, as said below
Outputs:
- new_table: float32 [262144, 400], P(('dp', 'blk'))
- new_sum: float32 [262144], P(('dp', 'blk'))
Inputs may be any that keep to these rules, and one draw needn't show every extreme that they name: `owner_map`: A permutation: every storage position appears once. The owner of position p is device p // 2048. `head_ids`: among the 128 heads, 128 tails and 512 negatives of one device taken together, at most 12 are stored on any one owner; in every draw 16 owners receive exactly 12 from every device. `tail_ids`: counted together with the heads and negatives of the same device, as stated for head_ids. `neg_ids`: counted together with the heads and tails of the same device, as stated for head_ids.
All inputs are finite; a program needn't handle non-finite values.
Results may differ from a plain program's by a relative error of at most 0.00005.
Values sent between devices are 32-bit elements; how exact they have to be, the bound alone decides.
A program may use at most 128 MiB of HBM per device.

v0:
```python
import jax
import jax.numpy as jnp
from jax import lax
from jax.sharding import PartitionSpec as P

MARGIN = 10.0
EPSILON = 1e-05
LEARNING_RATE = 0.1


def negative_terms(queries, neg_block, weight):
    query_sq = jnp.sum(queries * queries, axis=1)
    block_sq = jnp.sum(neg_block * neg_block, axis=1)
    inner_prod = jnp.dot(
        queries, neg_block.T, precision=lax.Precision.HIGHEST, preferred_element_type=jnp.float32
    )
    distance = jnp.sqrt(query_sq[:, None] + block_sq[None, :] - 2.0 * inner_prod + EPSILON)
    coefficient = -jax.nn.sigmoid(MARGIN - distance) / (weight * distance)
    grad_query = queries * jnp.sum(coefficient, axis=1)[:, None] - jnp.dot(
        coefficient, neg_block, precision=lax.Precision.HIGHEST, preferred_element_type=jnp.float32
    )
    grad_block = neg_block * jnp.sum(coefficient, axis=0)[:, None] - jnp.dot(
        coefficient.T, queries, precision=lax.Precision.HIGHEST, preferred_element_type=jnp.float32
    )
    return (grad_query, grad_block)


def send_requests(requests):
    return lax.all_to_all(requests, ("dp", "blk"), split_axis=0, concat_axis=0, tiled=True)


def move_rows(payload):
    return lax.all_to_all(payload, ("dp", "blk"), split_axis=0, concat_axis=0, tiled=True)


def on_device(
    entity_table, adagrad_sum, relations, owner_map, head_ids, rel_ids, tail_ids, neg_ids
):
    dp_count = lax.axis_size("dp")
    blk_count = lax.axis_size("blk")
    owner_count = dp_count * blk_count
    rows_here, width = entity_table.shape
    edge_count = head_ids.shape[0]
    neg_count = neg_ids.shape[0]
    request_count = 2 * edge_count + neg_count
    capacity = max(2, 2 * request_count // owner_count)
    wanted = jnp.concatenate([head_ids, tail_ids, neg_ids])
    position = owner_map[wanted]
    owner_of = position // rows_here
    local_row = position % rows_here
    onehot = (owner_of[:, None] == jnp.arange(owner_count, dtype=jnp.int32)[None, :]).astype(
        jnp.int32
    )
    before = jnp.cumsum(onehot, axis=0) - onehot
    rank_in = jnp.sum(before * onehot, axis=1)
    slot_of = owner_of * capacity + rank_in
    requests = jnp.zeros((owner_count * capacity,), jnp.int32).at[slot_of].set(local_row)
    requests = requests.reshape(owner_count, capacity)
    asked_rows = send_requests(requests)
    served = entity_table[asked_rows]
    fetched = move_rows(served).reshape(owner_count * capacity, width)[slot_of]
    head_rows = fetched[:edge_count]
    tail_rows = fetched[edge_count : 2 * edge_count]
    neg_block = fetched[2 * edge_count :]
    queries = head_rows + relations[rel_ids]
    residue = queries - tail_rows
    pos_dist = jnp.sqrt(jnp.sum(residue * residue, axis=1) + EPSILON)
    grad_pos = (jax.nn.sigmoid(pos_dist - MARGIN) / pos_dist)[:, None] * residue
    weight = float(blk_count * neg_count)
    part_query, part_block = negative_terms(
        queries, lax.all_gather(neg_block, "blk", axis=0, tiled=True), weight
    )
    block_grad = lax.psum_scatter(part_block, "blk", scatter_dimension=0, tiled=True)
    gradients = jnp.concatenate([grad_pos + part_query, -grad_pos, block_grad])
    outgoing = jnp.zeros((owner_count * capacity, width), jnp.float32).at[slot_of].set(gradients)
    incoming = move_rows(outgoing.reshape(owner_count, capacity, width))
    summed = (
        jnp.zeros_like(entity_table).at[asked_rows.reshape(-1)].add(incoming.reshape(-1, width))
    )
    new_sum = adagrad_sum + jnp.mean(summed * summed, axis=1)
    new_table = entity_table - LEARNING_RATE * summed / jnp.sqrt(new_sum)[:, None]
    return (new_table, new_sum)


def solution(mesh):
    return jax.shard_map(
        on_device,
        mesh=mesh,
        in_specs=(
            P(("dp", "blk"), None),
            P(("dp", "blk")),
            P(),
            P(),
            P(("dp", "blk")),
            P(("dp", "blk")),
            P(("dp", "blk")),
            P(("dp", "blk")),
        ),
        out_specs=(P(("dp", "blk"), None), P(("dp", "blk"))),
        check_vma=False,
    )
```

profile of v0, /device:TPU:1, one launch (start us, length us, event | category | flops | bytes accessed | tf_op | source)
XLA Modules:
  0.0 335.3 jit_solution(6407851075444210870)
XLA Ops:
  7.2 0.0 copy-start
  7.2 0.8 fusion.20
  8.0 0.4 copy-done
  8.4 4.5 %gather_fusion = s32[768]{0:T(1024)S(1)} fusion(s32[262144]{0:T(1024)S(1)} %copy-done, s32[1024]{0:T(1024)S(1)} %pad_clamp_fusion.3), kind=kCustom, calls=%fused_computation | custom fusion | bytes 9216 | tf_op jit(solution)/shard_map/gather | solution.py:48
  12.9 0.1 copy.29
  13.1 0.2 fusion.8
  13.3 0.1 copy.30
  13.4 0.3 fusion.11
  13.8 3.4 %scatter_custom_fusion = s32[1536]{0:T(1024)S(1)} fusion(s32[768]{0:T(1024)S(1)} %fusion.21, s32[768]{0:T(1024)S(1)} %get-tuple-element.15, s32[]{:T(128)} %constant.22.clone.1), kind=kCustom, calls=%fused_computation.64 | custom fusion | bytes 6148 | tf_op jit(solution)/shard_map/scatter | solution.py:57
  17.2 0.7 all_to_all.14
  17.9 11.5 %all-to-all-start = ((s32[128,1,12]{2,1,0:T(1,128)}), s32[128,1,12]{2,1,0:T(1,128)S(1)}, u32[]{:S(2)}, u32[]{:S(2)}) async-start(s32[128,1,12]{2,1,0:T(1,128)} %bitcast.7), calls=%async_computation | async-start | bytes 131072 | tf_op jit(solution)/shard_map/all_to_all | solution.py:29
  29.4 5.1 %copy.39 = f32[2048,400]{1,0:T(8,128)} copy(f32[2048,400]{0,1:T(8,128)} %param.8) | data formatting | bytes 6553600 | tf_op args[0]
  34.4 4.4 %all-to-all-done = s32[128,1,12]{2,1,0:T(1,128)S(1)} async-done(((s32[128,1,12]{2,1,0:T(1,128)}), s32[128,1,12]{2,1,0:T(1,128)S(1)}, u32[]{:S(2)}, u32[]{:S(2)}) %all-to-all-start) | async-done | bytes 6176 | tf_op jit(solution)/shard_map/all_to_all | solution.py:29
  38.8 0.1 reshape.314
  38.9 7.9 %gather_fusion.1 = f32[1536,400]{1,0:T(8,128)} fusion(f32[2048,400]{1,0:T(8,128)} %copy.39, s32[2048]{0:T(1024)S(1)} %pad_clamp_fusion), kind=kCustom, calls=%fused_computation.1 | custom fusion | bytes 4921344 | tf_op jit(solution)/shard_map/gather | solution.py:60
  46.8 4.6 %reshape.313 = f32[128,12,400]{2,1,0:T(8,128)} reshape(f32[1536,400]{1,0:T(8,128)} %gather_fusion.1) | data formatting | bytes 4915200 | tf_op jit(solution)/shard_map/gather | solution.py:60
  51.4 5.9 %all-to-all-start.1 = ((f32[128,12,400]{2,1,0:T(8,128)}), f32[128,12,400]{2,1,0:T(8,128)}, u32[]{:S(2)}, u32[]{:S(2)}) async-start(f32[128,12,400]{2,1,0:T(8,128)} %reshape.313), calls=%async_computation.1 | async-start | bytes 8388608 | tf_op jit(solution)/shard_map/all_to_all | solution.py:33
  57.2 0.0 all-gather.2.cloned.1.call-start
  57.3 52.5 %all-to-all-done.1 = f32[128,12,400]{2,1,0:T(8,128)} async-done(((f32[128,12,400]{2,1,0:T(8,128)}), f32[128,12,400]{2,1,0:T(8,128)}, u32[]{:S(2)}, u32[]{:S(2)}) %all-to-all-start.1) | async-done | bytes 2457632 | tf_op jit(solution)/shard_map/all_to_all | solution.py:33
  109.8 4.6 %reshape.301 = f32[1536,400]{1,0:T(8,128)} reshape(f32[128,12,400]{2,1,0:T(8,128)} %all-to-all-done.1) | data formatting | bytes 4915200 | tf_op jit(solution)/shard_map/reshape | solution.py:61
  114.4 4.7 %gather_fusion.2 = f32[768,400]{1,0:T(8,128)S(1)} fusion(f32[1536,400]{1,0:T(8,128)} %reshape.301, s32[1024]{0:T(1024)S(1)} %pad_clamp_fusion.2), kind=kCustom, calls=%fused_computation.2 | custom fusion | bytes 2460672 | tf_op jit(solution)/shard_map/gather | solution.py:61
  119.0 0.1 slice.31
  119.1 1.2 copy.43
  120.3 0.0 all-gather.2.cloned.1.call-update
  120.3 0.0 copy-start.5
  120.4 0.2 reduce-scatter.2.cloned.1.call-start
  120.6 14.2 %copy.34 = f32[7424,400]{1,0:T(8,128)} copy(f32[7424,400]{0,1:T(8,128)} %param.10) | data formatting | bytes 23756800 | tf_op args[2]
  134.8 0.0 copy-done.5
  134.8 6.5 %gather_fusion.3 = f32[128,400]{1,0:T(8,128)S(1)} fusion(f32[7424,400]{1,0:T(8,128)} %copy.34, s32[1024]{0:T(1024)S(1)} %pad_clamp_fusion.1), kind=kCustom, calls=%fused_computation.3 | custom fusion | bytes 410112 | tf_op jit(solution)/shard_map/gather | solution.py:65
  141.3 0.1 copy.35
  141.5 0.1 copy.41
  141.6 0.1 copy.42
  141.8 0.1 multiply_reduce_fusion.3
  141.8 0.1 multiply_reduce_fusion.2
  141.9 18.3 %all-gather.2.cloned.1.call-done = f32[4096,400]{0,1:T(8,128)} async-done(((f32[512,400]{0,1:T(8,128)}), f32[4096,400]{0,1:T(8,128)}) %all-gather.2.cloned.1.call-update) | async-done | bytes 6553616 | tf_op jit(solution)/shard_map/all_gather | solution.py:71
  160.2 0.0 copy-start.3
  160.3 3.6 %multiply_reduce_fusion = f32[4096]{0:T(1024)S(1)} fusion(f32[4096,400]{0,1:T(8,128)} %all-gather.2.cloned.1.call-done), kind=kLoop, calls=%fused_computation.8 | loop fusion | flops 3272704 | bytes 6569984 | tf_op jit(solution)/shard_map/reduce_sum | solution.py:13
  163.9 1.1 copy-done.3
  165.0 5.5 %fusion.23 = (f32[128]{0:T(128)S(1)}, f32[4096]{0:T(1024)S(1)}, f32[128,4096]{1,0:T(8,128)S(1)}) fusion(f32[128,400]{0,1:T(8,128)S(1)} %get-tuple-element.12, f32[4096,400]{0,1:T(8,128)S(1)} %copy-done.3, f32[4096]{0:T(1024)S(1)} %multiply_reduce_fusion, f32[128]{0:T(128)S(1)} %multiply_reduce_fusion.2), kind=kOutput, calls=%fused_computation.73 | convolution fusion | flops 2523394048 | bytes 8889344 | tf_op jit(solution)/shard_map/dot_general | solution.py:14
  170.5 7.6 %multiply_subtract_fusion = f32[4096,400]{0,1:T(8,128)} fusion(f32[4096,400]{0,1:T(8,128)S(1)} %copy-done.3, f32[128,4096]{1,0:T(8,128)S(1)} %get-tuple-element.17, f32[128,400]{0,1:T(8,128)S(1)} %get-tuple-element.12, f32[4096]{0:T(1024)S(1)} %get-tuple-element.7), kind=kOutput, calls=%fused_computation.7 | convolution fusion | flops 2519859200 | bytes 15425536 | tf_op jit(solution)/shard_map/dot_general | solution.py:22
  178.1 0.0 reduce-scatter.2.cloned.1.call-update
  178.2 7.6 %fusion.7 = f32[128,400]{0,1:T(8,128)S(1)} fusion(f32[128,4096]{1,0:T(8,128)S(1)} %get-tuple-element.17, f32[4096,400]{0,1:T(8,128)} %all-gather.2.cloned.1.call-done, f32[128,400]{0,1:T(8,128)S(1)} %get-tuple-element.12, f32[128,400]{0,1:T(8,128)S(1)} %get-tuple-element.11, f32[128]{0:T(128)S(1)} %get-tuple-element.6, f32[128]{0:T(128)S(1)} %multiply_divide_fusion.1), kind=kOutput, calls=%fused_computation.22 | convolution fusion | flops 2516787200 | bytes 9266176 | tf_op jit(solution)/shard_map/dot_general | solution.py:19
  185.8 35.3 %reduce-scatter.2.cloned.1.call-done = f32[512,400]{0,1:T(8,128)} async-done(((f32[4096,400]{0,1:T(8,128)}), f32[512,400]{0,1:T(8,128)}) %reduce-scatter.2.cloned.1.call-update) | async-done | bytes 819216 | tf_op jit(solution)/shard_map/reduce_scatter | solution.py:73
  221.1 1.2 pad_maximum_fusion
  222.3 1.6 copy.38
  223.9 8.0 %scatter_custom_fusion.1 = f32[1536,400]{1,0:T(8,128)} fusion(s32[768]{0:T(1024)S(1)} %fusion.21, f32[768,400]{1,0:T(8,128)} %copy.38, f32[]{:T(128)} %constant.21.clone.1), kind=kCustom, calls=%fused_computation.18 | custom fusion | bytes 2458112 | tf_op jit(solution)/shard_map/scatter | solution.py:75
  232.0 4.6 %reshape.302 = f32[128,12,400]{2,1,0:T(8,128)} reshape(f32[1536,400]{1,0:T(8,128)} %scatter_custom_fusion.1) | data formatting | bytes 4915200 | tf_op jit(solution)/shard_map/reshape | solution.py:76
  236.5 8.9 %all-to-all-start.2 = ((f32[128,12,400]{2,1,0:T(8,128)}), f32[128,12,400]{2,1,0:T(8,128)}, u32[]{:S(2)}, u32[]{:S(2)}) async-start(f32[128,12,400]{2,1,0:T(8,128)} %reshape.302), calls=%async_computation.3 | async-start | bytes 8388608 | tf_op jit(solution)/shard_map/all_to_all | solution.py:33
  245.4 0.5 broadcast.247
  245.9 0.8 reduce.9
  246.7 0.1 reshape.300
  246.9 51.1 %all-to-all-done.2 = f32[128,12,400]{2,1,0:T(8,128)} async-done(((f32[128,12,400]{2,1,0:T(8,128)}), f32[128,12,400]{2,1,0:T(8,128)}, u32[]{:S(2)}, u32[]{:S(2)}) %all-to-all-start.2) | async-done | bytes 2457632 | tf_op jit(solution)/shard_map/all_to_all | solution.py:33
  297.9 4.6 %reshape.356 = f32[1536,400]{1,0:T(8,128)} reshape(f32[128,12,400]{2,1,0:T(8,128)} %all-to-all-done.2) | data formatting | bytes 4915200 | tf_op jit(solution)/shard_map/reshape | solution.py:78
  302.5 12.4 %scatter_custom_fusion.2 = f32[2048,400]{1,0:T(8,128)} fusion(s32[1536]{0:T(1024)S(1)} %fusion.13, f32[1536,400]{1,0:T(8,128)} %reshape.356, f32[]{:T(128)} %constant.21.clone.1), kind=kCustom, calls=%fused_computation.16 | custom fusion | flops 614400 | bytes 3277312 | tf_op jit(solution)/shard_map/scatter-add | solution.py:78
  314.9 0.0 copy-start.4
  314.9 0.0 copy-start.2
  314.9 2.7 multiply_reduce_fusion.1
  317.6 0.0 copy-done.4
  317.7 0.6 fusion.24
  318.3 0.1 copy-done.2
  318.4 0.0 copy-start.1
  318.4 4.9 %divide_subtract_fusion = f32[2048,400]{1,0:T(8,128)} fusion(f32[2048,400]{1,0:T(8,128)S(1)} %copy-done.2, f32[2048,400]{1,0:T(8,128)} %scatter_custom_fusion.2, f32[2048]{0:T(1024)S(1)} %get-tuple-element.8), kind=kLoop, calls=%fused_computation.13 | loop fusion | flops 2457600 | bytes 9838592 | tf_op jit(solution)/shard_map/sub | solution.py:81
  323.3 5.2 %copy.40 = f32[2048,400]{0,1:T(8,128)} copy(f32[2048,400]{1,0:T(8,128)} %divide_subtract_fusion) | data formatting | bytes 6553600
  328.5 0.0 copy-done.1
  (16 shorter events, 0.3 us)
Async XLA Ops:
  7.2 1.3 copy-start
  17.9 20.9 %all-to-all-start = ((s32[128,1,12]{2,1,0:T(1,128)}), s32[128,1,12]{2,1,0:T(1,128)S(1)}, u32[]{:S(2)}, u32[]{:S(2)}) async-start(s32[128,1,12]{2,1,0:T(1,128)} %bitcast.7), calls=%async_computation | async-start | bytes 131072 | tf_op jit(solution)/shard_map/all_to_all | solution.py:29
  51.4 58.4 %all-to-all-start.1 = ((f32[128,12,400]{2,1,0:T(8,128)}), f32[128,12,400]{2,1,0:T(8,128)}, u32[]{:S(2)}, u32[]{:S(2)}) async-start(f32[128,12,400]{2,1,0:T(8,128)} %reshape.313), calls=%async_computation.1 | async-start | bytes 8388608 | tf_op jit(solution)/shard_map/all_to_all | solution.py:33
  57.2 103.0 %all-gather.2.cloned.1.call-start = ((), (), s32[]{:S(2)}) async-start(), calls=%async_computation.4 | async-start | bytes 7372800 | tf_op jit(solution)/shard_map/all_gather | solution.py:71
  120.3 14.5 %copy-start.5 = (s32[128]{0:T(128)S(1)}, s32[128]{0:T(128)}, u32[]{:S(2)}) copy-start(s32[128]{0:T(128)} %param.13) | copy-start | bytes 1540
  120.4 100.7 %reduce-scatter.2.cloned.1.call-start = ((), (), s32[]{:S(2)}) async-start(), calls=%async_computation.5 | async-start | bytes 7372800 | tf_op jit(solution)/shard_map/reduce_scatter | solution.py:73
  160.2 4.7 %copy-start.3 = (f32[4096,400]{0,1:T(8,128)S(1)}, f32[4096,400]{0,1:T(8,128)}, u32[]{:S(2)}) copy-start(f32[4096,400]{0,1:T(8,128)} %all-gather.2.cloned.1.call-done) | copy-start | bytes 19660804
  236.5 61.4 %all-to-all-start.2 = ((f32[128,12,400]{2,1,0:T(8,128)}), f32[128,12,400]{2,1,0:T(8,128)}, u32[]{:S(2)}, u32[]{:S(2)}) async-start(f32[128,12,400]{2,1,0:T(8,128)} %reshape.302), calls=%async_computation.3 | async-start | bytes 8388608 | tf_op jit(solution)/shard_map/all_to_all | solution.py:33
  314.9 2.7 copy-start.4
  314.9 3.5 %copy-start.2 = (f32[2048,400]{1,0:T(8,128)S(1)}, f32[2048,400]{1,0:T(8,128)}, u32[]{:S(2)}) copy-start(f32[2048,400]{1,0:T(8,128)} %copy.39) | copy-start | bytes 9830404
  318.4 10.1 %copy-start.1 = (s32[262144]{0:T(1024)S(1)}, s32[262144]{0:T(1024)}, u32[]{:S(2)}) copy-start(s32[262144]{0:T(1024)} %param.11) | copy-start | bytes 3145732
Sparse Core Ops, SparseCore 0:
  120.5 39.7 all-gather.1
  178.3 42.7 reduce-scatter.1
where the time goes:
time: 337 us; the launch traced here: 335 us
  waiting for transfers between devices  162 us (48%)
  local copies, waits for them, and re-layouts  84.3 us (25%)
  other arithmetic  28 us (8%)
  starting transfers between devices  26.5 us (8%)
  matrix products  20.8 us (6%)
  between operations  14.3 us (4%)
    all_to_all x2, waiting for transfers between devices, move_rows(): lax.all_to_all(payload, ('dp', 'blk'), split_axis=0, concat_axis=0, tiled...  104 us
    reduce_scatter x1, waiting for transfers between devices, on_device(): lax.psum_scatter(part_block, 'blk', scatter_dimension=0, tiled=True)  35.3 us
    unnamed x18, local copies, waits for them, and re-layouts  27.6 us
    all_gather x1, waiting for transfers between devices, on_device(): lax.all_gather(neg_block, 'blk', axis=0, tiled=True)  18.3 us
    all_to_all x2, starting transfers between devices, move_rows(): lax.all_to_all(payload, ('dp', 'blk'), split_axis=0, concat_axis=0, tiled...  14.7 us
    gather x2, local copies, waits for them, and re-layouts, on_device(): served = entity_table[asked_rows]  12.4 us
    scatter-add x1, other arithmetic, on_device(): jnp.zeros_like(entity_table).at[asked_rows.reshape(-1)]  12.4 us
    all_to_all x1, starting transfers between devices, send_requests(): lax.all_to_all(requests, ('dp', 'blk'), split_axis=0, concat_axis=0, tile...  11.5 us
  transfers between devices with their start and end apart: 5, of which 5 were waited for; matrix products, arithmetic and copies ran while one was open for 11% of the time, Pallas kernels for 0%

commit v1 on v0

--- a/solution.py
+++ b/solution.py
@@ -62,16 +62,21 @@
     head_rows = fetched[:edge_count]
     tail_rows = fetched[edge_count : 2 * edge_count]
     neg_block = fetched[2 * edge_count :]
-    queries = head_rows + relations[rel_ids]
+    pick = (rel_ids[:, None] == jnp.arange(relations.shape[0], dtype=jnp.int32)[None, :]).astype(
+        jnp.float32
+    )
+    rel_rows = jnp.dot(
+        pick, relations, precision=lax.Precision.HIGHEST, preferred_element_type=jnp.float32
+    )
+    queries = head_rows + rel_rows
     residue = queries - tail_rows
     pos_dist = jnp.sqrt(jnp.sum(residue * residue, axis=1) + EPSILON)
     grad_pos = (jax.nn.sigmoid(pos_dist - MARGIN) / pos_dist)[:, None] * residue
     weight = float(blk_count * neg_count)
-    part_query, part_block = negative_terms(
-        queries, lax.all_gather(neg_block, "blk", axis=0, tiled=True), weight
-    )
-    block_grad = lax.psum_scatter(part_block, "blk", scatter_dimension=0, tiled=True)
-    gradients = jnp.concatenate([grad_pos + part_query, -grad_pos, block_grad])
+    all_queries = lax.all_gather(queries, "blk", axis=0, tiled=True)
+    part_query, block_grad = negative_terms(all_queries, neg_block, weight)
+    grad_neg = lax.psum_scatter(part_query, "blk", scatter_dimension=0, tiled=True)
+    gradients = jnp.concatenate([grad_pos + grad_neg, -grad_pos, block_grad])
     outgoing = jnp.zeros((owner_count * capacity, width), jnp.float32).at[slot_of].set(gradients)
     incoming = move_rows(outgoing.reshape(owner_count, capacity, width))
     summed = (

time: 337 us -> 318 us (0.944)
  local copies, waits for them, and re-layouts: 84.3 us -> 65.5 us
  matrix products: 20.8 us -> 29.2 us
  waiting for transfers between devices: 162 us -> 154 us
    unnamed x18 -> x28, local copies, waits for them, and re-layouts: 27.6 us -> 15.5 us
    dot_general x0 -> x1, matrix products: none -> 9.85 us  [on_device(): jnp.dot(pick, relations, precision=lax.Precision.HIGHEST, preferred_eleme...]
    reduce_scatter x1, waiting for transfers between devices: 35.3 us -> 25.9 us  [on_device(): lax.psum_scatter(part_query, 'blk', scatter_dimension=0, tiled=True)]
    gather x2 -> x0, local copies, waits for them, and re-layouts: 6.6 us -> none  [on_device(): queries = head_rows + relations[rel_ids]]
    dot_general x1, matrix products: 5.5 us -> 10.6 us  [negative_terms(): jnp.dot(queries, neg_block.T, precision=lax.Precision.HIGHEST, preferred_...]
    reduce_sum x1, other arithmetic: 3.64 us -> 0.1 us  [negative_terms(): block_sq = jnp.sum(neg_block * neg_block, axis=1)]
    dot_general x1, matrix products: 7.63 us -> 4.12 us  [negative_terms(): jnp.dot(coefficient, neg_block, precision=lax.Precision.HIGHEST, preferre...]
  transfers between devices with their start and end apart: 5 -> 5, of which waited for: 5 -> 5; matrix products, arithmetic and copies ran while one was open for 11% -> 4% of each run, Pallas kernels for 0% -> 0%
where the time goes in v1:
time: 318 us; the launch traced here: 317 us
  waiting for transfers between devices  154 us (48%)
  local copies, waits for them, and re-layouts  65.5 us (21%)
  matrix products  29.2 us (9%)
  starting transfers between devices  28 us (9%)
  other arithmetic  25.7 us (8%)
  between operations  14.3 us (4%)
    all_to_all x2, waiting for transfers between devices, move_rows(): lax.all_to_all(payload, ('dp', 'blk'), split_axis=0, concat_axis=0, tiled...  104 us
    reduce_scatter x1, waiting for transfers between devices, on_device(): lax.psum_scatter(part_query, 'blk', scatter_dimension=0, tiled=True)  25.9 us
    all_gather x1, waiting for transfers between devices, on_device(): all_queries = lax.all_gather(queries, 'blk', axis=0, tiled=True)  20.4 us
    all_to_all x2, starting transfers between devices, move_rows(): lax.all_to_all(payload, ('dp', 'blk'), split_axis=0, concat_axis=0, tiled...  16.3 us
    unnamed x28, local copies, waits for them, and re-layouts  15.5 us
    scatter-add x1, other arithmetic, on_device(): jnp.zeros_like(entity_table).at[asked_rows.reshape(-1)]  12.4 us
    gather x2, local copies, waits for them, and re-layouts, on_device(): served = entity_table[asked_rows]  12.4 us
    all_to_all x1, starting transfers between devices, send_requests(): lax.all_to_all(requests, ('dp', 'blk'), split_axis=0, concat_axis=0, tile...  11.5 us
  transfers between devices with their start and end apart: 5, of which 5 were waited for; matrix products, arithmetic and copies ran while one was open for 4% of the time, Pallas kernels for 0%

profile of v1, /device:TPU:1, one launch (start us, length us, event | category | flops | bytes accessed | tf_op | source)
XLA Modules:
  0.0 317.0 jit_solution(2606483320302243880)
XLA Ops:
  7.2 0.0 copy-start
  7.2 0.8 fusion.19
  8.0 0.4 copy-done
  8.4 4.5 %gather_fusion = s32[768]{0:T(1024)S(1)} fusion(s32[262144]{0:T(1024)S(1)} %copy-done, s32[1024]{0:T(1024)S(1)} %pad_clamp_fusion.2), kind=kCustom, calls=%fused_computation | custom fusion | bytes 9216 | tf_op jit(solution)/shard_map/gather | solution.py:48
  12.9 0.1 copy.25
  13.1 0.2 fusion.7
  13.3 0.1 copy.26
  13.4 0.3 fusion.10
  13.8 3.4 %scatter_custom_fusion = s32[1536]{0:T(1024)S(1)} fusion(s32[768]{0:T(1024)S(1)} %fusion.20, s32[768]{0:T(1024)S(1)} %get-tuple-element.16, s32[]{:T(128)} %constant.22.clone.1), kind=kCustom, calls=%fused_computation.62 | custom fusion | bytes 6148 | tf_op jit(solution)/shard_map/scatter | solution.py:57
  17.2 0.7 all_to_all.14
  17.9 11.5 %all-to-all-start = ((s32[128,1,12]{2,1,0:T(1,128)}), s32[128,1,12]{2,1,0:T(1,128)S(1)}, u32[]{:S(2)}, u32[]{:S(2)}) async-start(s32[128,1,12]{2,1,0:T(1,128)} %bitcast.7), calls=%async_computation | async-start | bytes 131072 | tf_op jit(solution)/shard_map/all_to_all | solution.py:29
  29.4 5.0 %copy.33 = f32[2048,400]{1,0:T(8,128)} copy(f32[2048,400]{0,1:T(8,128)} %param.8) | data formatting | bytes 6553600 | tf_op args[0]
  34.4 4.4 %all-to-all-done = s32[128,1,12]{2,1,0:T(1,128)S(1)} async-done(((s32[128,1,12]{2,1,0:T(1,128)}), s32[128,1,12]{2,1,0:T(1,128)S(1)}, u32[]{:S(2)}, u32[]{:S(2)}) %all-to-all-start) | async-done | bytes 6176 | tf_op jit(solution)/shard_map/all_to_all | solution.py:29
  38.8 0.6 copy-done.7
  39.4 0.1 reshape.315
  39.5 7.9 %gather_fusion.1 = f32[1536,400]{1,0:T(8,128)} fusion(f32[2048,400]{1,0:T(8,128)} %copy.33, s32[2048]{0:T(1024)S(1)} %pad_clamp_fusion), kind=kCustom, calls=%fused_computation.1 | custom fusion | bytes 4921344 | tf_op jit(solution)/shard_map/gather | solution.py:60
  47.4 4.5 %reshape.314 = f32[128,12,400]{2,1,0:T(8,128)} reshape(f32[1536,400]{1,0:T(8,128)} %gather_fusion.1) | data formatting | bytes 4915200 | tf_op jit(solution)/shard_map/gather | solution.py:60
  52.0 5.8 %all-to-all-start.1 = ((f32[128,12,400]{2,1,0:T(8,128)}), f32[128,12,400]{2,1,0:T(8,128)}, u32[]{:S(2)}, u32[]{:S(2)}) async-start(f32[128,12,400]{2,1,0:T(8,128)} %reshape.314), calls=%async_computation.1 | async-start | bytes 8388608 | tf_op jit(solution)/shard_map/all_to_all | solution.py:33
  57.8 0.0 all-gather.2.cloned.1.call-start
  57.8 52.5 %all-to-all-done.1 = f32[128,12,400]{2,1,0:T(8,128)} async-done(((f32[128,12,400]{2,1,0:T(8,128)}), f32[128,12,400]{2,1,0:T(8,128)}, u32[]{:S(2)}, u32[]{:S(2)}) %all-to-all-start.1) | async-done | bytes 2457632 | tf_op jit(solution)/shard_map/all_to_all | solution.py:33
  110.3 4.6 %reshape.302 = f32[1536,400]{1,0:T(8,128)} reshape(f32[128,12,400]{2,1,0:T(8,128)} %all-to-all-done.1) | data formatting | bytes 4915200 | tf_op jit(solution)/shard_map/reshape | solution.py:61
  114.9 4.7 %gather_fusion.2 = f32[768,400]{1,0:T(8,128)S(1)} fusion(f32[1536,400]{1,0:T(8,128)} %reshape.302, s32[1024]{0:T(1024)S(1)} %pad_clamp_fusion.1), kind=kCustom, calls=%fused_computation.2 | custom fusion | bytes 2460672 | tf_op jit(solution)/shard_map/gather | solution.py:61
  119.6 0.0 copy-start.4
  119.6 0.1 copy.36
  119.8 0.1 copy.35
  119.9 0.0 copy-done.10
  119.9 9.8 %multiply_reduce_fusion.3 = (f32[128]{0:T(128)S(1)}, f32[128,400]{0,1:T(8,128)S(1)}, f32[128,400]{0,1:T(8,128)}) fusion(f32[128,400]{0,1:T(8,128)S(1)} %copy.36, f32[128,400]{0,1:T(8,128)S(1)} %copy.35, f32[7424,400]{0,1:T(8,128)} %param.10, s32[128]{0:T(128)S(1)} %copy-done.10), kind=kOutput, calls=%fused_computation.31 | convolution fusion | flops 4562460672 | bytes 12698624 | tf_op jit(solution)/shard_map/dot_general | solution.py:68
  129.8 0.0 all-gather.2.cloned.1.call-update
  129.8 0.2 reduce-scatter.2.cloned.1.call-start
  130.0 0.0 copy-done.4
  130.0 1.0 slice.29
  131.1 1.5 copy.37
  132.6 0.1 multiply_reduce_fusion.2
  132.7 20.4 %all-gather.2.cloned.1.call-done = f32[1024,400]{0,1:T(8,128)} async-done(((f32[128,400]{0,1:T(8,128)}), f32[1024,400]{0,1:T(8,128)}) %all-gather.2.cloned.1.call-update) | async-done | bytes 1638416 | tf_op jit(solution)/shard_map/all_gather | solution.py:76
  153.1 1.6 multiply_reduce_fusion.1
  154.6 0.0 copy-start.5
  154.6 10.6 %fusion.24 = (f32[1024]{0:T(1024)S(1)}, f32[512]{0:T(512)S(1)}, f32[1024,512]{1,0:T(8,128)S(1)}) fusion(f32[1024,400]{0,1:T(8,128)} %all-gather.2.cloned.1.call-done, f32[768,400]{1,0:T(8,128)} %copy-done.4, f32[512]{0:T(512)S(1)} %multiply_reduce_fusion.2, f32[1024]{0:T(1024)S(1)} %multiply_reduce_fusion.1), kind=kOutput, calls=%fused_computation.72 | convolution fusion | flops 2523396608 | bytes 4796416 | tf_op jit(solution)/shard_map/dot_general | solution.py:14
  165.2 0.0 copy-start.6
  165.2 1.3 copy-done.6
  166.5 0.0 copy-done.3
  166.5 0.0 copy-done.5
  166.5 4.1 %multiply_subtract_fusion = f32[1024,400]{0,1:T(8,128)} fusion(f32[1024,400]{0,1:T(8,128)S(1)} %copy-done.3, f32[1024,512]{1,0:T(8,128)S(1)} %get-tuple-element.18, f32[1024]{0:T(1024)S(1)} %get-tuple-element.6, f32[768,400]{1,0:T(8,128)S(1)} %copy-done.5), kind=kOutput, calls=%fused_computation.14 | convolution fusion | flops 2517401600 | bytes 6426624 | tf_op jit(solution)/shard_map/dot_general | solution.py:19
  170.6 0.0 reduce-scatter.2.cloned.1.call-update
  170.7 4.7 %convolution_subtract_fusion = f32[512,400]{0,1:T(8,128)S(1)} fusion(f32[1024,512]{1,0:T(8,128)} %copy-done.6, f32[1024,400]{0,1:T(8,128)S(1)} %copy-done.3, f32[512,400]{0,1:T(8,128)S(1)} %copy.37, f32[512]{0:T(512)S(1)} %get-tuple-element.7), kind=kOutput, calls=%fused_computation.18 | convolution fusion | flops 2516992000 | bytes 5376000 | tf_op jit(solution)/shard_map/dot_general | solution.py:22
  175.4 25.9 %reduce-scatter.2.cloned.1.call-done = f32[128,400]{0,1:T(8,128)} async-done(((f32[1024,400]{0,1:T(8,128)}), f32[128,400]{0,1:T(8,128)}) %reduce-scatter.2.cloned.1.call-update) | async-done | bytes 204816 | tf_op jit(solution)/shard_map/reduce_scatter | solution.py:78
  201.3 1.0 multiply_add_fusion
  202.2 0.1 pad_maximum_fusion
  202.3 1.6 copy.32
  204.0 8.0 %scatter_custom_fusion.1 = f32[1536,400]{1,0:T(8,128)} fusion(s32[768]{0:T(1024)S(1)} %fusion.20, f32[768,400]{1,0:T(8,128)} %copy.32, f32[]{:T(128)} %constant.21.clone.1), kind=kCustom, calls=%fused_computation.16 | custom fusion | bytes 2458112 | tf_op jit(solution)/shard_map/scatter | solution.py:80
  212.0 4.5 %reshape.303 = f32[128,12,400]{2,1,0:T(8,128)} reshape(f32[1536,400]{1,0:T(8,128)} %scatter_custom_fusion.1) | data formatting | bytes 4915200 | tf_op jit(solution)/shard_map/reshape | solution.py:81
  216.5 10.5 %all-to-all-start.2 = ((f32[128,12,400]{2,1,0:T(8,128)}), f32[128,12,400]{2,1,0:T(8,128)}, u32[]{:S(2)}, u32[]{:S(2)}) async-start(f32[128,12,400]{2,1,0:T(8,128)} %reshape.303), calls=%async_computation.3 | async-start | bytes 8388608 | tf_op jit(solution)/shard_map/all_to_all | solution.py:33
  227.0 0.5 broadcast.244
  227.5 0.0 copy-done.8
  227.5 0.8 reduce.9
  228.3 0.1 reshape.301
  228.5 51.1 %all-to-all-done.2 = f32[128,12,400]{2,1,0:T(8,128)} async-done(((f32[128,12,400]{2,1,0:T(8,128)}), f32[128,12,400]{2,1,0:T(8,128)}, u32[]{:S(2)}, u32[]{:S(2)}) %all-to-all-start.2) | async-done | bytes 2457632 | tf_op jit(solution)/shard_map/all_to_all | solution.py:33
  279.5 4.6 %reshape.349 = f32[1536,400]{1,0:T(8,128)} reshape(f32[128,12,400]{2,1,0:T(8,128)} %all-to-all-done.2) | data formatting | bytes 4915200 | tf_op jit(solution)/shard_map/reshape | solution.py:83
  284.1 12.4 %scatter_custom_fusion.2 = f32[2048,400]{1,0:T(8,128)} fusion(s32[1536]{0:T(1024)S(1)} %fusion.12, f32[1536,400]{1,0:T(8,128)} %reshape.349, f32[]{:T(128)} %constant.21.clone.1), kind=kCustom, calls=%fused_computation.11 | custom fusion | flops 614400 | bytes 3277312 | tf_op jit(solution)/shard_map/scatter-add | solution.py:83
  296.6 2.7 multiply_reduce_fusion
  299.3 0.0 copy-done.9
  299.3 0.6 fusion.25
  299.9 0.1 copy-done.2
  300.0 5.0 %divide_subtract_fusion = f32[2048,400]{1,0:T(8,128)} fusion(f32[2048,400]{1,0:T(8,128)S(1)} %copy-done.2, f32[2048,400]{1,0:T(8,128)} %scatter_custom_fusion.2, f32[2048]{0:T(1024)S(1)} %get-tuple-element.8), kind=kLoop, calls=%fused_computation.6 | loop fusion | flops 2457600 | bytes 9838592 | tf_op jit(solution)/shard_map/sub | solution.py:86
  305.0 5.2 %copy.34 = f32[2048,400]{0,1:T(8,128)} copy(f32[2048,400]{1,0:T(8,128)} %divide_subtract_fusion) | data formatting | bytes 6553600
  (21 shorter events, 0.2 us)
Async XLA Ops:
  7.2 1.3 copy-start
  17.9 20.9 %all-to-all-start = ((s32[128,1,12]{2,1,0:T(1,128)}), s32[128,1,12]{2,1,0:T(1,128)S(1)}, u32[]{:S(2)}, u32[]{:S(2)}) async-start(s32[128,1,12]{2,1,0:T(1,128)} %bitcast.7), calls=%async_computation | async-start | bytes 131072 | tf_op jit(solution)/shard_map/all_to_all | solution.py:29
  38.8 0.6 copy-start.7
  52.0 58.3 %all-to-all-start.1 = ((f32[128,12,400]{2,1,0:T(8,128)}), f32[128,12,400]{2,1,0:T(8,128)}, u32[]{:S(2)}, u32[]{:S(2)}) async-start(f32[128,12,400]{2,1,0:T(8,128)} %reshape.314), calls=%async_computation.1 | async-start | bytes 8388608 | tf_op jit(solution)/shard_map/all_to_all | solution.py:33
  57.8 95.3 %all-gather.2.cloned.1.call-start = ((), (), s32[]{:S(2)}) async-start(), calls=%async_computation.4 | async-start | bytes 1843200 | tf_op jit(solution)/shard_map/all_gather | solution.py:76
  114.9 5.0 %copy-start.10 = (s32[128]{0:T(128)S(1)}, s32[128]{0:T(128)}, u32[]{:S(2)}) copy-start(s32[128]{0:T(128)} %param.13) | copy-start | bytes 1540
  119.6 10.4 %copy-start.4 = (f32[768,400]{1,0:T(8,128)}, f32[768,400]{1,0:T(8,128)S(1)}, u32[]{:S(2)}) copy-start(f32[768,400]{1,0:T(8,128)S(1)} %gather_fusion.2) | copy-start | bytes 3686404
  129.8 71.5 %reduce-scatter.2.cloned.1.call-start = ((), (), s32[]{:S(2)}) async-start(), calls=%async_computation.5 | async-start | bytes 1843200 | tf_op jit(solution)/shard_map/reduce_scatter | solution.py:78
  154.6 11.9 %copy-start.3 = (f32[1024,400]{0,1:T(8,128)S(1)}, f32[1024,400]{0,1:T(8,128)}, u32[]{:S(2)}) copy-start(f32[1024,400]{0,1:T(8,128)} %all-gather.2.cloned.1.call-done) | copy-start | bytes 4915204
  154.6 11.9 %copy-start.5 = (f32[768,400]{1,0:T(8,128)S(1)}, f32[768,400]{1,0:T(8,128)}, u32[]{:S(2)}) copy-start(f32[768,400]{1,0:T(8,128)} %copy-done.4) | copy-start | bytes 3686404
  165.2 1.3 copy-start.6
  216.5 11.0 %copy-start.8 = (s32[128,1,12]{2,1,0:T(1,128)S(1)}, s32[128,1,12]{2,1,0:T(1,128)}, u32[]{:S(2)}) copy-start(s32[128,1,12]{2,1,0:T(1,128)} %copy-done.7) | copy-start | bytes 18436
  216.5 63.0 %all-to-all-start.2 = ((f32[128,12,400]{2,1,0:T(8,128)}), f32[128,12,400]{2,1,0:T(8,128)}, u32[]{:S(2)}, u32[]{:S(2)}) async-start(f32[128,12,400]{2,1,0:T(8,128)} %reshape.303), calls=%async_computation.3 | async-start | bytes 8388608 | tf_op jit(solution)/shard_map/all_to_all | solution.py:33
  296.6 2.7 copy-start.9
  296.6 3.5 %copy-start.2 = (f32[2048,400]{1,0:T(8,128)S(1)}, f32[2048,400]{1,0:T(8,128)}, u32[]{:S(2)}) copy-start(f32[2048,400]{1,0:T(8,128)} %copy.33) | copy-start | bytes 9830404
  300.0 10.1 %copy-start.1 = (s32[262144]{0:T(1024)S(1)}, s32[262144]{0:T(1024)}, u32[]{:S(2)}) copy-start(s32[262144]{0:T(1024)} %param.11) | copy-start | bytes 3145732
Sparse Core Ops, SparseCore 0:
  129.9 23.1 all-gather.1
  170.8 30.4 reduce-scatter.1

commit v2 on v0

v2 whole, which is shorter than its diff:
```python
import functools

import jax
import jax.numpy as jnp
from jax import lax
from jax.experimental import pallas as pl
from jax.experimental.pallas import tpu as pltpu
from jax.sharding import PartitionSpec as P

MARGIN = 10.0
EPSILON = 1e-05
LEARNING_RATE = 0.1
MESH = pl.DeviceIdType.MESH
F32 = jnp.float32
BF16 = jnp.bfloat16
DEVICES = 128
CAP = 12
PAD = 16
GROUP = 16
CHUNKS = DEVICES // GROUP
SLOTS = GROUP * PAD
LINES = 40
LANES = 128
TAIL = 16


def split(x):
    high = x.astype(BF16)
    return high, (x - high.astype(F32)).astype(BF16)


def dot(a, b, ca, cb):
    return lax.dot_general(a, b, (((ca,), (cb,)), ((), ())), preferred_element_type=F32)


def dot3(a, b, ca, cb):
    return dot(a[0], b[0], ca, cb) + (dot(a[0], b[1], ca, cb) + dot(a[1], b[0], ca, cb))


def iota(shape, axis):
    return lax.broadcasted_iota(jnp.int32, shape, axis)


def onehot(mask):
    return jnp.where(mask, 1.0, 0.0).astype(BF16)


def to_column(row):
    n = row.shape[1]
    return jnp.sum(jnp.where(iota((n, n), 0) == iota((n, n), 1), row, 0.0), axis=1, keepdims=True)


def to_row(column):
    n = column.shape[0]
    return jnp.sum(jnp.where(iota((n, n), 0) == iota((n, n), 1), column, 0.0), axis=0, keepdims=True)


def tail_mask():
    return iota((GROUP, 8, LANES), 1) == iota((GROUP, 8, LANES), 2) // TAIL


def pack(buffer, c, full):
    full = full.reshape(GROUP, PAD, 4 * LANES)
    up, low = full[:, 0:8], full[:, 8:16]
    sub = iota((GROUP, 8, LANES), 1)
    first = sub < 4
    tail_up = jnp.sum(jnp.where(tail_mask(), up[:, :, 3 * LANES :], 0.0), axis=1, keepdims=True)
    tail_low = jnp.sum(
        jnp.where(tail_mask() & first, low[:, :, 3 * LANES :], 0.0), axis=1, keepdims=True
    )
    here = pl.ds(c * GROUP, GROUP)
    for n in range(3):
        buffer[here, 8 * n : 8 * n + 8, :] = up[:, :, LANES * n : LANES * n + LANES]
    buffer[here, 24:32, :] = jnp.where(first, low[:, :, 0:LANES], low[:, :, LANES : 2 * LANES])
    rest = jnp.where(sub == 4, tail_up, jnp.where(sub == 5, tail_low, 0.0))
    buffer[here, 32:40, :] = jnp.where(first, low[:, :, 2 * LANES : 3 * LANES], rest)


def unpack(buffer, c):
    part = buffer[pl.ds(c * GROUP, GROUP)]
    lines = [part[:, 8 * n : 8 * n + 8] for n in range(5)]
    first = iota((GROUP, 8, LANES), 1) < 4
    tail_up = jnp.where(tail_mask(), lines[4][:, 4:5], 0.0)
    tail_low = jnp.where(tail_mask() & first, lines[4][:, 5:6], 0.0)
    turned = pltpu.roll(lines[3].reshape(GROUP * 8, LANES), GROUP * 8 - 4, 0)
    turned = turned.reshape(GROUP, 8, LANES)
    up = jnp.concatenate([lines[0], lines[1], lines[2], tail_up], axis=2)
    low = jnp.concatenate([lines[3], turned, lines[4], tail_low], axis=2)
    return jnp.concatenate([up, low], axis=1).reshape(SLOTS, 4 * LANES)


def step_kernel(
    heads,
    tails,
    negs,
    rels,
    map_hbm,
    table_hbm,
    relations_hbm,
    adagrad,
    table_out,
    sum_out,
    map_ref,
    table,
    relations,
    map_parts,
    table_high,
    table_low,
    ids,
    key_col,
    local_col,
    slot_col,
    slot_row,
    ask_send,
    asked,
    index_col,
    row_send,
    rows,
    wanted,
    rel_rows,
    neg_pieces,
    block_acc,
    coef_cols,
    all_queries,
    part_own,
    part_other,
    part_sibling,
    part_sum,
    part_recv,
    grad_pieces,
    grad_send,
    grads,
    summed,
    load_sem,
    ask_sems,
    row_sems,
    grad_sems,
    query_sems,
    part_sems,
    send_sems,
    query_send_sems,
    part_send_sems,
):
    dp = lax.axis_index("dp")
    blk = lax.axis_index("blk")
    mx, mz = dp // 4, lax.rem(dp, 4)
    my, mc = blk // 2, lax.rem(blk, 2)
    width = table.shape[0]
    body = 3 * LANES
    rows_here = table.shape[1]
    edges = heads.shape[1]

    def deltas(i):
        a, b, c, dc = lax.rem(i, 4), lax.rem(i // 4, 4), lax.rem(i // 16, 4), i // 64
        return a, lax.rem(a + b, 4), lax.rem(a + c, 4), dc

    def ahead(i):
        dx, dy, dz, dc = deltas(i)
        return (
            lax.rem(mx + dx, 4) * 4 + lax.rem(mz + dz, 4),
            lax.rem(my + dy, 4) * 2 + lax.rem(mc + dc, 2),
        )

    def behind(i):
        dx, dy, dz, dc = deltas(i)
        return (
            lax.rem(mx + 4 - dx, 4) * 4 + lax.rem(mz + 4 - dz, 4),
            lax.rem(my + 4 - dy, 4) * 2 + lax.rem(mc + dc, 2),
        )

    def remote(src, dst, send, recv, device):
        return pltpu.make_async_remote_copy(
            src_ref=src,
            dst_ref=dst,
            send_sem=send,
            recv_sem=recv,
            device_id=device,
            device_id_type=MESH,
        )

    load_map = pltpu.make_async_copy(map_hbm, map_ref, load_sem.at[0])
    load_table = pltpu.make_async_copy(table_hbm, table, load_sem.at[1])
    load_relations = pltpu.make_async_copy(relations_hbm, relations, load_sem.at[2])
    load_map.start()
    load_table.start()
    load_relations.start()
    barrier = pltpu.get_barrier_semaphore()

    @pl.loop(1, DEVICES)
    def _(i):
        pl.semaphore_signal(barrier, inc=1, device_id=ahead(i), device_id_type=MESH)

    ids[0:1, :] = heads[...]
    ids[1:2, :] = tails[...]
    ids[2:6, :] = negs[...]
    load_map.wait()
    position_of = map_ref[...]
    map_parts[:, 0:128] = (position_of & 255).astype(F32).astype(BF16)
    map_parts[:, 128:256] = ((position_of >> 8) & 255).astype(F32).astype(BF16)
    map_parts[:, 256:384] = (position_of >> 16).astype(F32).astype(BF16)

    @pl.loop(0, 6)
    def _(t):
        column = to_column(ids[pl.ds(t, 1), :].astype(F32)).astype(jnp.int32)
        line = onehot((column >> 7) == iota((128, map_ref.shape[0]), 1))
        found = dot(line, map_parts[...], 1, 0)
        lane = (column & 127) == iota((128, 128), 1)
        piece = [
            jnp.sum(jnp.where(lane, found[:, 128 * p : 128 * p + 128], 0.0), axis=1, keepdims=True)
            for p in range(3)
        ]
        position = (piece[0] + 256.0 * piece[1] + 65536.0 * piece[2]).astype(jnp.int32)
        owner = position >> 11
        dx = ((owner >> 5) - mx) & 3
        dz = ((owner >> 3) - mz) & 3
        dy = ((owner >> 1) - my) & 3
        dc = (owner - mc) & 1
        key = dc * 64 + ((dz - dx) & 3) * 16 + ((dy - dx) & 3) * 4 + dx
        where = pl.ds(pl.multiple_of(t * 128, 128), 128)
        key_col[where, :] = key.astype(F32)
        local_col[where, :] = (position & (rows_here - 1)).astype(F32)

    count = key_col.shape[0]
    keys = key_col[...]
    key_hot = onehot(keys.astype(jnp.int32) == iota((count, DEVICES), 1))
    earlier = onehot(iota((count, count), 1) < iota((count, count), 0))
    before = dot(earlier, key_hot, 1, 0)
    rank = jnp.sum(before * key_hot.astype(F32), axis=1, keepdims=True)
    local = local_col[...].astype(jnp.int32)
    place = rank.astype(jnp.int32)
    lane = iota((count, LANES), 1)
    spot = (place == lane) | ((place >= 8) & (place + 4 == lane))
    upper = jnp.where(spot, (local >> 8).astype(F32), 0.0).astype(BF16)
    lower = jnp.where(spot, (local & 255).astype(F32), 0.0).astype(BF16)
    asks = 256.0 * dot(key_hot, upper, 0, 0) + dot(key_hot, lower, 0, 0)
    ask_send[...] = asks.reshape(DEVICES, 1, 128)
    slot = keys * float(PAD) + rank
    slot_col[...] = slot
    for t in range(6):
        slot_row[t : t + 1, :] = to_row(slot[128 * t : 128 * t + 128])

    load_table.wait()
    high, low = split(table[...])
    table_high[0:width] = high
    table_low[0:width] = low
    for j in range(1, LANES // TAIL):
        table_high[body + TAIL * j : body + TAIL * j + TAIL] = high[body:]
        table_low[body + TAIL * j : body + TAIL * j + TAIL] = low[body:]
    summed[...] = jnp.zeros_like(summed)
    wanted[...] = jnp.zeros_like(wanted)
    asked[0] = ask_send[0]

    pl.semaphore_wait(barrier, DEVICES - 1)

    def ask_copy(i):
        return remote(
            ask_send.at[i], asked.at[i], send_sems.at[0], ask_sems.at[i // GROUP], ahead(i)
        )

    @pl.loop(1, DEVICES)
    def _(i):
        ask_copy(i).start()

    def wait_chunk(buffer, sems, c):
        @pl.when(c == 0)
        def _():
            part = buffer.at[pl.ds(1, GROUP - 1)]
            pltpu.make_async_copy(part, part, sems.at[0]).wait()

        @pl.when(c > 0)
        def _():
            part = buffer.at[pl.ds(c * GROUP, GROUP)]
            pltpu.make_async_copy(part, part, sems.at[c]).wait()

    def row_copy(i):
        return remote(
            row_send.at[i],
            rows.at[i],
            send_sems.at[1],
            row_sems.at[i // GROUP],
            behind(i),
        )

    @pl.loop(0, CHUNKS)
    def _(c):
        wait_chunk(asked, ask_sems, c)
        part = jnp.broadcast_to(asked[pl.ds(c * GROUP, GROUP)], (GROUP, PAD, 128))
        part = part.reshape(SLOTS, 128)
        index = jnp.sum(
            jnp.where(lax.rem(iota((SLOTS, 128), 0), PAD) == iota((SLOTS, 128), 1), part, 0.0),
            axis=1,
            keepdims=True,
        )
        index_col[pl.ds(pl.multiple_of(c * SLOTS, SLOTS), SLOTS), :] = index
        pick = onehot(index.astype(jnp.int32) == iota((SLOTS, rows_here), 1))
        picked = dot(pick, table_high[...], 1, 1) + dot(pick, table_low[...], 1, 1)
        pack(row_send, c, picked)

        @pl.when(c == 0)
        def _():
            rows[0] = row_send[0]

        @pl.loop(0, GROUP)
        def _(g):
            @pl.when(c * GROUP + g > 0)
            def _():
                row_copy(c * GROUP + g).start()

    load_relations.wait()
    rel_column = to_column(rels[...].astype(F32)).astype(jnp.int32)
    rel_rows[...] = jnp.zeros_like(rel_rows)

    @pl.loop(0, relations.shape[1] // 256)
    def _(t):
        high, low = split(relations[:, pl.ds(pl.multiple_of(t * 256, 256), 256)])
        pick = onehot(rel_column - t * 256 == iota((edges, 256), 1))
        rel_rows[:, 0:width] += dot(pick, high, 1, 1) + dot(pick, low, 1, 1)

    @pl.loop(0, CHUNKS)
    def _(c):
        wait_chunk(rows, row_sems, c)
        high, low = split(unpack(rows, c))
        place = onehot(slot_col[...].astype(jnp.int32) - c * SLOTS == iota((count, SLOTS), 1))
        wanted[...] += dot(place, high, 1, 0) + dot(place, low, 1, 0)

    high, low = split(wanted[:, body:])
    fold = onehot(lax.rem(iota((LANES, LANES), 0), TAIL) == iota((LANES, LANES), 1))
    wanted[:, body:] = dot(high, fold, 1, 0) + dot(low, fold, 1, 0)
    queries = wanted[0:edges, :] + rel_rows[...]
    residue = queries - wanted[edges : 2 * edges, :]
    pos_dist = jnp.sqrt(jnp.sum(residue * residue, axis=1, keepdims=True) + EPSILON)
    grad_pos = (1.0 / (1.0 + jnp.exp(MARGIN - pos_dist)) / pos_dist) * residue
    all_queries[0, 0] = queries

    sibling = (dp, blk + 1 - 2 * mc)

    def query_copy(dy):
        return remote(
            all_queries.at[0, 0],
            all_queries.at[dy, 0],
            query_send_sems.at[dy, 0],
            query_sems.at[dy, 0],
            (dp, lax.rem(my + dy, 4) * 2 + mc),
        )

    def forward_copy(dy):
        return remote(
            all_queries.at[dy, 0],
            all_queries.at[dy, 1],
            query_send_sems.at[dy, 1],
            query_sems.at[dy, 1],
            sibling,
        )

    for dy in (1, 3, 2):
        query_copy(dy).start()

    negatives = wanted[2 * edges :, :]
    high, low = split(negatives)
    neg_pieces[0] = high
    neg_pieces[1] = low
    neg_col = jnp.sum(negatives * negatives, axis=1, keepdims=True)
    neg_count = negatives.shape[0]
    neg_sq = jnp.concatenate(
        [to_row(neg_col[128 * t : 128 * t + 128]) for t in range(neg_count // 128)], axis=1
    )
    block_acc[...] = jnp.zeros_like(block_acc)
    coef_cols[...] = jnp.zeros_like(coef_cols)
    weight = 8.0 * neg_count

    def order(t):
        return t + (t // 2) * (1 - 2 * lax.rem(t, 2))

    def sibling_copy(dy):
        return remote(
            part_other.at[dy],
            part_sibling.at[dy],
            part_send_sems.at[dy, 0],
            part_sems.at[dy, 0],
            sibling,
        )

    def home_copy(dy):
        return remote(
            part_sum.at[dy],
            part_recv.at[dy],
            part_send_sems.at[dy, 1],
            part_sems.at[dy, 1],
            (dp, lax.rem(my + 4 - dy, 4) * 2 + mc),
        )

    def block_terms(block):
        pieces = split(block)
        block_sq = jnp.sum(block * block, axis=1, keepdims=True)
        neg_parts = (neg_pieces[0], neg_pieces[1])
        inner = dot3(pieces, neg_parts, 1, 1)
        dist = jnp.sqrt(block_sq + neg_sq - 2.0 * inner + EPSILON)
        coef = -1.0 / ((1.0 + jnp.exp(dist - MARGIN)) * (weight * dist))
        coef_parts = split(coef)
        coef_cols[...] += jnp.sum(coef, axis=0, keepdims=True)
        block_acc[...] += dot3(coef_parts, pieces, 0, 0)
        return block * jnp.sum(coef, axis=1, keepdims=True) - dot3(coef_parts, neg_parts, 1, 0)

    def finish(dy):
        sibling_copy(dy).wait_recv()
        part_sum[dy] = part_own[dy] + part_sibling[dy]

    @pl.loop(0, 4)
    def _(t):
        dy = order(t)

        @pl.when(t > 0)
        def _():
            query_copy(dy).wait_recv()

        forward_copy(dy).start()
        part_own[dy] = block_terms(all_queries[dy, 0])
        forward_copy(dy).wait_recv()
        part_other[dy] = block_terms(all_queries[dy, 1])
        sibling_copy(dy).start()

        @pl.when(t > 1)
        def _():
            last = order(t - 1)
            finish(last)
            home_copy(last).start()

    finish(2)
    home_copy(2).start()
    finish(0)
    for dy in (1, 3, 2):
        home_copy(dy).wait_recv()
    grad_neg = (part_sum[0] + part_recv[1]) + (part_recv[2] + part_recv[3])
    high, low = split(grad_pos + grad_neg)
    grad_pieces[0, 0:edges] = high
    grad_pieces[1, 0:edges] = low
    high, low = split(-grad_pos)
    grad_pieces[0, edges : 2 * edges] = high
    grad_pieces[1, edges : 2 * edges] = low
    coef_col = jnp.concatenate(
        [to_column(coef_cols[:, 128 * t : 128 * t + 128]) for t in range(neg_count // 128)], axis=0
    )
    high, low = split(wanted[2 * edges :, :] * coef_col - block_acc[...])
    grad_pieces[0, 2 * edges :] = high
    grad_pieces[1, 2 * edges :] = low

    spread = onehot(iota((LANES, LANES), 0) == lax.rem(iota((LANES, LANES), 1), TAIL))
    for n in range(2):
        grad_pieces[n, :, body:] = dot(grad_pieces[n, :, body:], spread, 1, 0).astype(BF16)

    def grad_copy(i):
        return remote(
            grad_send.at[i],
            grads.at[i],
            send_sems.at[2],
            grad_sems.at[i // GROUP],
            ahead(i),
        )

    @pl.loop(0, CHUNKS)
    def _(c):
        line = iota((SLOTS, LANES), 0)
        base = line + c * SLOTS - jnp.where(lax.rem(line, PAD) < CAP, 0, PAD - CAP)
        place = jnp.concatenate(
            [onehot(slot_row[t : t + 1, :].astype(jnp.int32) == base) for t in range(6)], axis=1
        )
        packed = dot(place, grad_pieces[0], 1, 0) + dot(place, grad_pieces[1], 1, 0)
        pack(grad_send, c, packed)

        @pl.when(c == 0)
        def _():
            grads[0] = grad_send[0]

        @pl.loop(0, GROUP)
        def _(g):
            @pl.when(c * GROUP + g > 0)
            def _():
                grad_copy(c * GROUP + g).start()

    @pl.loop(0, CHUNKS)
    def _(c):
        wait_chunk(grads, grad_sems, c)
        high, low = split(unpack(grads, c).T)
        index = index_col[pl.ds(pl.multiple_of(c * SLOTS, SLOTS), SLOTS), :].astype(jnp.int32)
        used = lax.rem(iota((SLOTS, 1), 0), PAD) < CAP
        pick = onehot(jnp.where(used, index, -1) == iota((SLOTS, rows_here), 1))
        summed[...] += dot(high, pick, 1, 0) + dot(low, pick, 1, 0)

    tail = summed[body:width]
    for j in range(1, LANES // TAIL):
        tail = tail + summed[body + TAIL * j : body + TAIL * j + TAIL]
    total = jnp.concatenate([summed[0:body], tail], axis=0)
    new_sum = adagrad[...] + jnp.sum(total * total, axis=0, keepdims=True) * (1.0 / width)
    sum_out[...] = new_sum
    table_out[...] = table[...] - total * (LEARNING_RATE / jnp.sqrt(new_sum))

    part = ask_send.at[pl.ds(1, DEVICES - 1)]
    pltpu.make_async_copy(part, part, send_sems.at[0]).wait()
    for n, buffer in ((1, row_send), (2, grad_send)):
        part = buffer.at[pl.ds(1, DEVICES - 1)]
        pltpu.make_async_copy(part, part, send_sems.at[n]).wait()
    for dy in range(4):
        forward_copy(dy).wait_send()
        sibling_copy(dy).wait_send()
        if dy > 0:
            query_copy(dy).wait_send()
            home_copy(dy).wait_send()


def on_device(entity_table, adagrad_sum, relations, owner_map, head_ids, rel_ids, tail_ids, neg_ids):
    rows_here, width = entity_table.shape
    edges = head_ids.shape[0]
    neg_count = neg_ids.shape[0]
    count = 2 * edges + neg_count
    map_rows = owner_map.shape[0] // 128
    vmem = pl.BlockSpec(memory_space=pltpu.VMEM)
    hbm = pl.BlockSpec(memory_space=pl.ANY)
    wide = 4 * LANES
    slots = pltpu.VMEM((DEVICES, LINES, LANES), F32)
    parts = pltpu.VMEM((4, edges, wide), F32)
    sem = pltpu.SemaphoreType.DMA
    new_table, new_sum = pl.pallas_call(
        step_kernel,
        out_shape=(
            jax.ShapeDtypeStruct((width, rows_here), F32),
            jax.ShapeDtypeStruct((1, rows_here), F32),
        ),
        in_specs=[vmem, vmem, vmem, vmem, hbm, hbm, hbm, vmem],
        out_specs=(vmem, vmem),
        scratch_shapes=[
            pltpu.VMEM((map_rows, 128), jnp.int32),
            pltpu.VMEM((width, rows_here), F32),
            pltpu.VMEM((width, relations.shape[0]), F32),
            pltpu.VMEM((map_rows, 384), BF16),
            pltpu.VMEM((wide, rows_here), BF16),
            pltpu.VMEM((wide, rows_here), BF16),
            pltpu.VMEM((8, 128), jnp.int32),
            pltpu.VMEM((count, 1), F32),
            pltpu.VMEM((count, 1), F32),
            pltpu.VMEM((count, 1), F32),
            pltpu.VMEM((8, 128), F32),
            pltpu.VMEM((DEVICES, 1, 128), F32),
            pltpu.VMEM((DEVICES, 1, 128), F32),
            pltpu.VMEM((DEVICES * PAD, 1), F32),
            slots,
            slots,
            pltpu.VMEM((count, wide), F32),
            pltpu.VMEM((edges, wide), F32),
            pltpu.VMEM((2, neg_count, wide), BF16),
            pltpu.VMEM((neg_count, wide), F32),
            pltpu.VMEM((1, neg_count), F32),
            pltpu.VMEM((4, 2, edges, wide), F32),
            parts,
            parts,
            parts,
            parts,
            parts,
            pltpu.VMEM((2, count, wide), BF16),
            slots,
            slots,
            pltpu.VMEM((wide, rows_here), F32),
            sem((3,)),
            sem((CHUNKS,)),
            sem((CHUNKS,)),
            sem((CHUNKS,)),
            sem((4, 2)),
            sem((4, 2)),
            sem((3,)),
            sem((4, 2)),
            sem((4, 2)),
        ],
        compiler_params=pltpu.CompilerParams(
            collective_id=0, has_side_effects=True, vmem_limit_bytes=64000000
        ),
    )(
        head_ids.reshape(1, edges),
        tail_ids.reshape(1, edges),
        neg_ids.reshape(neg_count // 128, 128),
        rel_ids.reshape(1, edges),
        owner_map.reshape(map_rows, 128),
        entity_table.T,
        relations.T,
        adagrad_sum.reshape(1, rows_here),
    )
    return new_table.T, new_sum.reshape(rows_here)


def solution(mesh):
    assert dict(mesh.shape) == {"dp": 16, "blk": 8}
    return jax.shard_map(
        on_device,
        mesh=mesh,
        in_specs=(
            P(("dp", "blk"), None),
            P(("dp", "blk")),
            P(),
            P(),
            P(("dp", "blk")),
            P(("dp", "blk")),
            P(("dp", "blk")),
            P(("dp", "blk")),
        ),
        out_specs=(P(("dp", "blk"), None), P(("dp", "blk"))),
        check_vma=False,
    )
```

time: 337 us -> 138 us (0.41)
  waiting for transfers between devices: 162 us -> 0 us
  Pallas kernels: 0 us -> 133 us
  local copies, waits for them, and re-layouts: 84.3 us -> 4.62 us
  other arithmetic: 28 us -> 0 us
  starting transfers between devices: 26.5 us -> 0 us
  matrix products: 20.8 us -> 0 us
  between operations: 14.3 us -> 0.65 us
    pallas_call x0 -> x1, Pallas kernels: none -> 133 us  [on_device(): pl.pallas_call(step_kernel, out_shape=(jax.ShapeDtypeStruct((width, rows_...]
    all_to_all x3 -> x0, waiting for transfers between devices: 108 us -> none  [the longest x2 104 us: move_rows(): lax.all_to_all(payload, ('dp', 'blk'), split_axis=0, concat_axis=0, tiled...]
    reduce_scatter x1 -> x0, waiting for transfers between devices: 35.3 us -> none  [on_device(): lax.psum_scatter(part_block, 'blk', scatter_dimension=0, tiled=True)]
    gather x6 -> x0, local copies, waits for them, and re-layouts: 28.1 us -> none  [the longest x2 12.4 us: on_device(): served = entity_table[asked_rows]]
    all_to_all x3 -> x0, starting transfers between devices: 26.2 us -> none  [the longest x2 14.7 us: move_rows(): lax.all_to_all(payload, ('dp', 'blk'), split_axis=0, concat_axis=0, tiled...]
    unnamed x18 -> x4, local copies, waits for them, and re-layouts: 27.6 us -> 4.62 us
    dot_general x3 -> x0, matrix products: 20.8 us -> none  [the longest x1 7.63 us: negative_terms(): jnp.dot(coefficient, neg_block, precision=lax.Precision.HIGHEST, preferre...]
    all_gather x1 -> x0, waiting for transfers between devices: 18.3 us -> none  [on_device(): lax.all_gather(neg_block, 'blk', axis=0, tiled=True)]
  transfers between devices with their start and end apart: 5 -> 0, of which waited for: 5 -> 0; matrix products, arithmetic and copies ran while one was open for 11% -> 0% of each run, Pallas kernels for 0% -> 0%
where the time goes in v2:
time: 138 us
  Pallas kernels  133 us (96%)
  local copies, waits for them, and re-layouts  4.62 us (3%)
    pallas_call x1, Pallas kernels, on_device(): pl.pallas_call(step_kernel, out_shape=(jax.ShapeDtypeStruct((width, rows_...  133 us
    unnamed x4, local copies, waits for them, and re-layouts  4.62 us

profile of v2, /device:TPU:1, one launch (start us, length us, event | category | flops | bytes accessed | tf_op | source)
XLA Modules:
  0.0 138.1 jit_solution(4657829798996484123)
XLA Ops:
  0.6 132.8 %shard_map.95 = (f32[400,2048]{1,0:T(8,128)}, f32[1,2048]{1,0:T(1,128)}) custom-call(s32[1,128]{1,0:T(1,128)} %bitcast.17, s32[1,128]{1,0:T(1,128)} %bitcast.18, s32[4,128]{1,0:T(4,128)} %bitcast.16, s32[1,128]{1,0:T(1,128)} %bitcast.19, s32[2048,128]{1,0:T(8,128)} %bitcast.13, f32[400,2048]{1,0:T(8,128)} %bitcast.12, f32[400,7424]{1,0:T(8,128)} %bitcast.10, ...), custom_call_target="tpu_custom_call" | custom-call | tf_op jit(solution)/shard_map/pallas_call | solution.py:522
  133.4 0.0 copy-start
  133.4 4.0 %copy.12 = f32[2048,400]{0,1:T(8,128)} copy(f32[2048,400]{0,1:T(8,128)} %bitcast.11) | data formatting | bytes 6553600
  137.5 0.0 copy-done
  137.5 0.6 copy.13
Async XLA Ops:
  133.4 4.0 %copy-start = (f32[1,2048]{1,0:T(1,128)S(1)}, f32[1,2048]{1,0:T(1,128)}, u32[]{:S(2)}) copy-start(f32[1,2048]{1,0:T(1,128)} %get-tuple-element.5) | copy-start | bytes 24580

commit v3 on v2

--- a/solution.py
+++ b/solution.py
@@ -20,8 +20,11 @@
 CHUNKS = DEVICES // GROUP
 SLOTS = GROUP * PAD
 LINES = 40
+LIMIT = 48 * 1024 * 1024
 LANES = 128
 TAIL = 16
+REL = 256
+REL_PARTS = 3
 
 
 def split(x):
@@ -87,6 +90,24 @@
     up = jnp.concatenate([lines[0], lines[1], lines[2], tail_up], axis=2)
     low = jnp.concatenate([lines[3], turned, lines[4], tail_low], axis=2)
     return jnp.concatenate([up, low], axis=1).reshape(SLOTS, 4 * LANES)
+
+
+def to_lines(x):
+    tail = x[:, 3 * LANES :]
+    for shift in (TAIL, 2 * TAIL, 4 * TAIL):
+        tail = tail + pltpu.roll(tail, shift, 1)
+    tail = tail.reshape(GROUP, 8, LANES)
+    tail = jnp.sum(jnp.where(tail_mask(), tail, 0.0), axis=1)
+    return jnp.concatenate([x[:, LANES * n : LANES * n + LANES] for n in range(3)] + [tail], axis=0)
+
+
+def from_lines(lines):
+    tail = lines[3 * LANES :].reshape(GROUP, 1, LANES)
+    tail = jnp.where(tail_mask(), tail, 0.0).reshape(LANES, LANES)
+    for shift in (4 * TAIL, 2 * TAIL, TAIL):
+        tail = tail + pltpu.roll(tail, shift, 1)
+    tail = jnp.where(iota((LANES, LANES), 1) < TAIL, tail, 0.0)
+    return jnp.concatenate([lines[LANES * n : LANES * n + LANES] for n in range(3)] + [tail], axis=1)
 
 
 def step_kernel(
@@ -108,15 +129,19 @@
     table_low,
     ids,
     key_col,
+    ask_col,
     local_col,
     slot_col,
     slot_row,
     ask_send,
+    ask_mid,
+    ask_sum,
     asked,
     index_col,
     row_send,
     rows,
     wanted,
+    rel_acc,
     rel_rows,
     neg_pieces,
     block_acc,
@@ -149,6 +174,9 @@
     body = 3 * LANES
     rows_here = table.shape[1]
     edges = heads.shape[1]
+    rel_chunks = relations_hbm.shape[1] // REL
+    rel_step = relations.shape[1] // REL
+    rel_cuts = [min(n * rel_step, rel_chunks) for n in range(REL_PARTS + 1)]
 
     def deltas(i):
         a, b, c, dc = lax.rem(i, 4), lax.rem(i // 4, 4), lax.rem(i // 16, 4), i // 64
@@ -180,15 +208,30 @@
 
     load_map = pltpu.make_async_copy(map_hbm, map_ref, load_sem.at[0])
     load_table = pltpu.make_async_copy(table_hbm, table, load_sem.at[1])
-    load_relations = pltpu.make_async_copy(relations_hbm, relations, load_sem.at[2])
+
+    def load_relations(half):
+        first, lanes = rel_cuts[half] * REL, (rel_cuts[half + 1] - rel_cuts[half]) * REL
+        part = relations_hbm.at[:, pl.ds(first, lanes)]
+        return pltpu.make_async_copy(part, relations.at[:, pl.ds(0, lanes)], load_sem.at[2])
+
     load_map.start()
     load_table.start()
-    load_relations.start()
+    load_relations(0).start()
     barrier = pltpu.get_barrier_semaphore()
 
-    @pl.loop(1, DEVICES)
-    def _(i):
-        pl.semaphore_signal(barrier, inc=1, device_id=ahead(i), device_id_type=MESH)
+    def in_group(r):
+        return dp, lax.rem(my + lax.rem(r, 4), 4) * 2 + lax.rem(mc + r // 4, 2)
+
+    def in_plane(p):
+        return lax.rem(mx + p // 4, 4) * 4 + lax.rem(mz + lax.rem(p, 4), 4), blk
+
+    @pl.loop(1, 8)
+    def _(r):
+        pl.semaphore_signal(barrier, inc=1, device_id=in_group(r), device_id_type=MESH)
+
+    @pl.loop(1, 16)
+    def _(p):
+        pl.semaphore_signal(barrier, inc=1, device_id=in_plane(p), device_id_type=MESH)
 
     ids[0:1, :] = heads[...]
     ids[1:2, :] = tails[...]
@@ -216,24 +259,27 @@
         dy = ((owner >> 1) - my) & 3
         dc = (owner - mc) & 1
         key = dc * 64 + ((dz - dx) & 3) * 16 + ((dy - dx) & 3) * 4 + dx
+        ask = (dc * 4 + dy) * 16 + dx * 4 + dz
         where = pl.ds(pl.multiple_of(t * 128, 128), 128)
         key_col[where, :] = key.astype(F32)
+        ask_col[where, :] = ask.astype(F32)
         local_col[where, :] = (position & (rows_here - 1)).astype(F32)
 
     count = key_col.shape[0]
     keys = key_col[...]
-    key_hot = onehot(keys.astype(jnp.int32) == iota((count, DEVICES), 1))
+    key_hot = onehot(ask_col[...].astype(jnp.int32) == iota((count, DEVICES), 1))
     earlier = onehot(iota((count, count), 1) < iota((count, count), 0))
     before = dot(earlier, key_hot, 1, 0)
     rank = jnp.sum(before * key_hot.astype(F32), axis=1, keepdims=True)
     local = local_col[...].astype(jnp.int32)
     place = rank.astype(jnp.int32)
     lane = iota((count, LANES), 1)
-    spot = (place == lane) | ((place >= 8) & (place + 4 == lane))
+    spread = lane - (ask_col[...].astype(jnp.int32) // 16) * PAD
+    spot = (place == spread) | ((place >= 8) & (place + 4 == spread))
     upper = jnp.where(spot, (local >> 8).astype(F32), 0.0).astype(BF16)
     lower = jnp.where(spot, (local & 255).astype(F32), 0.0).astype(BF16)
     asks = 256.0 * dot(key_hot, upper, 0, 0) + dot(key_hot, lower, 0, 0)
-    ask_send[...] = asks.reshape(DEVICES, 1, 128)
+    ask_send[...] = asks.reshape(8, 16, 1, LANES)
     slot = keys * float(PAD) + rank
     slot_col[...] = slot
     for t in range(6):
@@ -248,18 +294,31 @@
         table_low[body + TAIL * j : body + TAIL * j + TAIL] = low[body:]
     summed[...] = jnp.zeros_like(summed)
     wanted[...] = jnp.zeros_like(wanted)
-    asked[0] = ask_send[0]
-
-    pl.semaphore_wait(barrier, DEVICES - 1)
-
-    def ask_copy(i):
-        return remote(
-            ask_send.at[i], asked.at[i], send_sems.at[0], ask_sems.at[i // GROUP], ahead(i)
-        )
-
-    @pl.loop(1, DEVICES)
-    def _(i):
-        ask_copy(i).start()
+    ask_mid[0] = ask_send[0]
+
+    pl.semaphore_wait(barrier, 22)
+
+    def group_ask(r):
+        return remote(ask_send.at[r], ask_mid.at[r], send_sems.at[0], ask_sems.at[0], in_group(r))
+
+    def plane_ask(p):
+        return remote(ask_sum.at[p], asked.at[p], send_sems.at[3], ask_sems.at[1], in_plane(p))
+
+    @pl.loop(1, 8)
+    def _(r):
+        group_ask(r).start()
+
+    part = ask_mid.at[pl.ds(1, 7)]
+    pltpu.make_async_copy(part, part, ask_sems.at[0]).wait()
+    ask_sum[...] = jnp.sum(ask_mid[...], axis=0)
+
+    @pl.loop(1, 16)
+    def _(p):
+        plane_ask(p).start()
+
+    asked[0] = ask_sum[0]
+    part = asked.at[pl.ds(1, 15)]
+    pltpu.make_async_copy(part, part, ask_sems.at[1]).wait()
 
     def wait_chunk(buffer, sems, c):
         @pl.when(c == 0)
@@ -283,14 +342,13 @@
 
     @pl.loop(0, CHUNKS)
     def _(c):
-        wait_chunk(asked, ask_sems, c)
-        part = jnp.broadcast_to(asked[pl.ds(c * GROUP, GROUP)], (GROUP, PAD, 128))
-        part = part.reshape(SLOTS, 128)
-        index = jnp.sum(
-            jnp.where(lax.rem(iota((SLOTS, 128), 0), PAD) == iota((SLOTS, 128), 1), part, 0.0),
-            axis=1,
-            keepdims=True,
-        )
+        parts = []
+        for g in range(GROUP):
+            dx, dy, dz, dc = deltas(c * GROUP + g)
+            line = jnp.broadcast_to(asked[dx * 4 + dz], (PAD, LANES))
+            lane = iota((PAD, LANES), 1) - (dc * 4 + dy) * PAD
+            parts.append(jnp.where(lane == iota((PAD, LANES), 0), line, 0.0))
+        index = jnp.sum(jnp.concatenate(parts, axis=0), axis=1, keepdims=True)
         index_col[pl.ds(pl.multiple_of(c * SLOTS, SLOTS), SLOTS), :] = index
         pick = onehot(index.astype(jnp.int32) == iota((SLOTS, rows_here), 1))
         picked = dot(pick, table_high[...], 1, 1) + dot(pick, table_low[...], 1, 1)
@@ -306,15 +364,23 @@
             def _():
                 row_copy(c * GROUP + g).start()
 
-    load_relations.wait()
-    rel_column = to_column(rels[...].astype(F32)).astype(jnp.int32)
+    rel_acc[...] = jnp.zeros_like(rel_acc)
+    for half in range(REL_PARTS):
+        load_relations(half).wait()
+
+        @pl.loop(0, rel_cuts[half + 1] - rel_cuts[half])
+        def _(t):
+            high, low = split(relations[:, pl.ds(pl.multiple_of(t * REL, REL), REL)])
+            base = (t + rel_cuts[half]) * REL
+            pick = onehot(iota((REL, edges), 0) + base == rels[...])
+            found = dot(jnp.concatenate([high, low], axis=0), pick, 1, 0)
+            rel_acc[...] += found[0:width] + found[width:]
+
+        if half + 1 < REL_PARTS:
+            load_relations(half + 1).start()
+
     rel_rows[...] = jnp.zeros_like(rel_rows)
-
-    @pl.loop(0, relations.shape[1] // 256)
-    def _(t):
-        high, low = split(relations[:, pl.ds(pl.multiple_of(t * 256, 256), 256)])
-        pick = onehot(rel_column - t * 256 == iota((edges, 256), 1))
-        rel_rows[:, 0:width] += dot(pick, high, 1, 1) + dot(pick, low, 1, 1)
+    rel_rows[:, 0:width] = rel_acc[...].T
 
     @pl.loop(0, CHUNKS)
     def _(c):
@@ -330,7 +396,7 @@
     residue = queries - wanted[edges : 2 * edges, :]
     pos_dist = jnp.sqrt(jnp.sum(residue * residue, axis=1, keepdims=True) + EPSILON)
     grad_pos = (1.0 / (1.0 + jnp.exp(MARGIN - pos_dist)) / pos_dist) * residue
-    all_queries[0, 0] = queries
+    all_queries[0, 0] = to_lines(queries)
 
     sibling = (dp, blk + 1 - 2 * mc)
 
@@ -352,9 +418,9 @@
             sibling,
         )
 
-    for dy in (1, 3, 2):
-        query_copy(dy).start()
-
+    query_copy(1).start()
+    query_copy(3).start()
+    forward_copy(0).start()
     negatives = wanted[2 * edges :, :]
     high, low = split(negatives)
     neg_pieces[0] = high
@@ -409,14 +475,22 @@
     def _(t):
         dy = order(t)
 
-        @pl.when(t > 0)
+        @pl.when(t == 1)
         def _():
-            query_copy(dy).wait_recv()
-
-        forward_copy(dy).start()
-        part_own[dy] = block_terms(all_queries[dy, 0])
+            query_copy(1).wait_recv()
+            forward_copy(1).start()
+            query_copy(3).wait_recv()
+            query_copy(2).start()
+            forward_copy(3).start()
+
+        @pl.when(t == 3)
+        def _():
+            query_copy(2).wait_recv()
+            forward_copy(2).start()
+
+        part_own[dy] = to_lines(block_terms(from_lines(all_queries[dy, 0])))
         forward_copy(dy).wait_recv()
-        part_other[dy] = block_terms(all_queries[dy, 1])
+        part_other[dy] = to_lines(block_terms(from_lines(all_queries[dy, 1])))
         sibling_copy(dy).start()
 
         @pl.when(t > 1)
@@ -430,7 +504,7 @@
     finish(0)
     for dy in (1, 3, 2):
         home_copy(dy).wait_recv()
-    grad_neg = (part_sum[0] + part_recv[1]) + (part_recv[2] + part_recv[3])
+    grad_neg = from_lines((part_sum[0] + part_recv[1]) + (part_recv[2] + part_recv[3]))
     high, low = split(grad_pos + grad_neg)
     grad_pieces[0, 0:edges] = high
     grad_pieces[1, 0:edges] = low
@@ -494,8 +568,10 @@
     sum_out[...] = new_sum
     table_out[...] = table[...] - total * (LEARNING_RATE / jnp.sqrt(new_sum))
 
-    part = ask_send.at[pl.ds(1, DEVICES - 1)]
+    part = ask_send.at[pl.ds(1, 7)]
     pltpu.make_async_copy(part, part, send_sems.at[0]).wait()
+    part = asked.at[pl.ds(1, 15)]
+    pltpu.make_async_copy(part, part, send_sems.at[3]).wait()
     for n, buffer in ((1, row_send), (2, grad_send)):
         part = buffer.at[pl.ds(1, DEVICES - 1)]
         pltpu.make_async_copy(part, part, send_sems.at[n]).wait()
@@ -517,7 +593,7 @@
     hbm = pl.BlockSpec(memory_space=pl.ANY)
     wide = 4 * LANES
     slots = pltpu.VMEM((DEVICES, LINES, LANES), F32)
-    parts = pltpu.VMEM((4, edges, wide), F32)
+    parts = pltpu.VMEM((4, width, LANES), F32)
     sem = pltpu.SemaphoreType.DMA
     new_table, new_sum = pl.pallas_call(
         step_kernel,
@@ -530,7 +606,7 @@
         scratch_shapes=[
             pltpu.VMEM((map_rows, 128), jnp.int32),
             pltpu.VMEM((width, rows_here), F32),
-            pltpu.VMEM((width, relations.shape[0]), F32),
+            pltpu.VMEM((width, -(-relations.shape[0] // (REL * REL_PARTS)) * REL), F32),
             pltpu.VMEM((map_rows, 384), BF16),
             pltpu.VMEM((wide, rows_here), BF16),
             pltpu.VMEM((wide, rows_here), BF16),
@@ -538,18 +614,22 @@
             pltpu.VMEM((count, 1), F32),
             pltpu.VMEM((count, 1), F32),
             pltpu.VMEM((count, 1), F32),
+            pltpu.VMEM((count, 1), F32),
             pltpu.VMEM((8, 128), F32),
-            pltpu.VMEM((DEVICES, 1, 128), F32),
-            pltpu.VMEM((DEVICES, 1, 128), F32),
+            pltpu.VMEM((8, 16, 1, LANES), F32),
+            pltpu.VMEM((8, 16, 1, LANES), F32),
+            pltpu.VMEM((16, 1, LANES), F32),
+            pltpu.VMEM((16, 1, LANES), F32),
             pltpu.VMEM((DEVICES * PAD, 1), F32),
             slots,
             slots,
             pltpu.VMEM((count, wide), F32),
+            pltpu.VMEM((width, edges), F32),
             pltpu.VMEM((edges, wide), F32),
             pltpu.VMEM((2, neg_count, wide), BF16),
             pltpu.VMEM((neg_count, wide), F32),
             pltpu.VMEM((1, neg_count), F32),
-            pltpu.VMEM((4, 2, edges, wide), F32),
+            pltpu.VMEM((4, 2, width, LANES), F32),
             parts,
             parts,
             parts,
@@ -560,17 +640,17 @@
             slots,
             pltpu.VMEM((wide, rows_here), F32),
             sem((3,)),
-            sem((CHUNKS,)),
+            sem((2,)),
             sem((CHUNKS,)),
             sem((CHUNKS,)),
             sem((4, 2)),
             sem((4, 2)),
-            sem((3,)),
+            sem((4,)),
             sem((4, 2)),
             sem((4, 2)),
         ],
         compiler_params=pltpu.CompilerParams(
-            collective_id=0, has_side_effects=True, vmem_limit_bytes=64000000
+            collective_id=0, has_side_effects=True, vmem_limit_bytes=LIMIT
         ),
     )(
         head_ids.reshape(1, edges),

time: 138 us -> 129 us (0.935)
  Pallas kernels: 133 us -> 120 us
  local copies, waits for them, and re-layouts: 4.62 us -> 6.87 us
    pallas_call x1, Pallas kernels: 133 us -> 120 us  [on_device(): pl.pallas_call(step_kernel, out_shape=(jax.ShapeDtypeStruct((width, rows_...]
    unnamed x4 -> x14, local copies, waits for them, and re-layouts: 4.62 us -> 6.87 us
where the time goes in v3:
time: 129 us; the launch traced here: 128 us
  Pallas kernels  120 us (93%)
  local copies, waits for them, and re-layouts  6.87 us (5%)
    pallas_call x1, Pallas kernels, on_device(): pl.pallas_call(step_kernel, out_shape=(jax.ShapeDtypeStruct((width, rows_...  120 us
    unnamed x14, local copies, waits for them, and re-layouts  6.87 us

profile of v3, /device:TPU:1, one launch (start us, length us, event | category | flops | bytes accessed | tf_op | source)
XLA Modules:
  0.0 128.0 jit_solution(11408729902808018135)
XLA Ops:
  0.6 0.0 copy-start
  0.6 1.2 copy-done
  1.9 0.0 copy-start.1
  1.9 0.7 copy-done.1
  2.6 0.0 copy-start.2
  2.6 0.7 copy-done.2
  3.2 0.0 copy-start.3
  3.2 0.7 copy-done.3
  3.9 0.0 copy-start.4
  3.9 0.7 copy-done.4
  4.5 0.0 copy-start.5
  4.6 0.7 copy-done.5
  5.2 120.4 %shard_map.95 = (f32[400,2048]{1,0:T(8,128)S(1)}, f32[1,2048]{1,0:T(1,128)S(1)}) custom-call(s32[1,128]{1,0:T(1,128)S(1)} %bitcast.15, s32[1,128]{1,0:T(1,128)S(1)} %bitcast.16, s32[4,128]{1,0:T(4,128)S(1)} %bitcast.14, s32[1,128]{1,0:T(1,128)S(1)} %bitcast.17, s32[2048,128]{1,0:T(8,128)S(1)} %bitcast.11, f32[400,2048]{1,0:T(8,128)} %bitcast.19, ...), custom_call_target="tpu_custom_call" | custom-call | tf_op jit(solution)/shard_map/pallas_call | solution.py:598
  125.7 1.7 %copy.12 = f32[2048,400]{0,1:T(8,128)} copy(f32[2048,400]{0,1:T(8,128)S(1)} %bitcast.10) | data formatting | bytes 6553600
  127.4 0.6 copy.13
Async XLA Ops:
  0.6 1.2 copy-start
  1.9 0.7 copy-start.1
  2.6 0.7 copy-start.2
  3.2 0.7 copy-start.3
  3.9 0.7 copy-start.4
  4.5 0.7 copy-start.5

commit v4 on v3

--- a/solution.py
+++ b/solution.py
@@ -111,16 +111,21 @@
 
 
 def step_kernel(
+    heads_hbm,
+    tails_hbm,
+    negs_hbm,
+    rels_hbm,
+    map_hbm,
+    table_hbm,
+    relations_hbm,
+    adagrad_hbm,
+    table_out,
+    sum_out,
     heads,
     tails,
     negs,
     rels,
-    map_hbm,
-    table_hbm,
-    relations_hbm,
     adagrad,
-    table_out,
-    sum_out,
     map_ref,
     table,
     relations,
@@ -147,8 +152,7 @@
     block_acc,
     coef_cols,
     all_queries,
-    part_own,
-    part_other,
+    parts,
     part_sibling,
     part_sum,
     part_recv,
@@ -160,9 +164,11 @@
     ask_sems,
     row_sems,
     grad_sems,
+    half_sems,
     query_sems,
     part_sems,
     send_sems,
+    half_send_sems,
     query_send_sems,
     part_send_sems,
 ):
@@ -214,6 +220,20 @@
         part = relations_hbm.at[:, pl.ds(first, lanes)]
         return pltpu.make_async_copy(part, relations.at[:, pl.ds(0, lanes)], load_sem.at[2])
 
+    small = [
+        pltpu.make_async_copy(src, dst, load_sem.at[3 + n])
+        for n, (src, dst) in enumerate(
+            [
+                (heads_hbm, heads),
+                (tails_hbm, tails),
+                (negs_hbm, negs),
+                (rels_hbm, rels),
+                (adagrad_hbm, adagrad),
+            ]
+        )
+    ]
+    for copy in small:
+        copy.start()
     load_map.start()
     load_table.start()
     load_relations(0).start()
@@ -233,6 +253,8 @@
     def _(p):
         pl.semaphore_signal(barrier, inc=1, device_id=in_plane(p), device_id_type=MESH)
 
+    for copy in small:
+        copy.wait()
     ids[0:1, :] = heads[...]
     ids[1:2, :] = tails[...]
     ids[2:6, :] = negs[...]
@@ -400,26 +422,40 @@
 
     sibling = (dp, blk + 1 - 2 * mc)
 
-    def query_copy(dy):
+    def at_y(dy):
+        return dp, lax.rem(my + dy, 4) * 2 + mc
+
+    def half_copy(dy, half):
+        lines = pl.ds(half * (width // 2), width // 2)
         return remote(
-            all_queries.at[0, 0],
-            all_queries.at[dy, 0],
-            query_send_sems.at[dy, 0],
-            query_sems.at[dy, 0],
-            (dp, lax.rem(my + dy, 4) * 2 + mc),
+            all_queries.at[0, 0, lines, :],
+            all_queries.at[dy, 0, lines, :],
+            half_send_sems.at[dy, half],
+            half_sems.at[dy, half],
+            at_y(dy),
+        )
+
+    def relay_copy(half):
+        lines = pl.ds(half * (width // 2), width // 2)
+        return remote(
+            all_queries.at[1 + 2 * half, 0, lines, :],
+            all_queries.at[2, 0, lines, :],
+            half_send_sems.at[2, half],
+            half_sems.at[2, half],
+            at_y(1 + 2 * half),
         )
 
     def forward_copy(dy):
         return remote(
             all_queries.at[dy, 0],
             all_queries.at[dy, 1],
-            query_send_sems.at[dy, 1],
-            query_sems.at[dy, 1],
+            query_send_sems.at[dy],
+            query_sems.at[dy],
             sibling,
         )
 
-    query_copy(1).start()
-    query_copy(3).start()
+    for dy, half in ((1, 0), (3, 1), (1, 1), (3, 0)):
+        half_copy(dy, half).start()
     forward_copy(0).start()
     negatives = wanted[2 * edges :, :]
     high, low = split(negatives)
@@ -434,12 +470,9 @@
     coef_cols[...] = jnp.zeros_like(coef_cols)
     weight = 8.0 * neg_count
 
-    def order(t):
-        return t + (t // 2) * (1 - 2 * lax.rem(t, 2))
-
     def sibling_copy(dy):
         return remote(
-            part_other.at[dy],
+            parts.at[dy, 1],
             part_sibling.at[dy],
             part_send_sems.at[dy, 0],
             part_sems.at[dy, 0],
@@ -469,33 +502,45 @@
 
     def finish(dy):
         sibling_copy(dy).wait_recv()
-        part_sum[dy] = part_own[dy] + part_sibling[dy]
-
-    @pl.loop(0, 4)
-    def _(t):
-        dy = order(t)
-
-        @pl.when(t == 1)
-        def _():
-            query_copy(1).wait_recv()
+        part_sum[dy] = parts[dy, 0] + part_sibling[dy]
+
+    @pl.loop(0, 8)
+    def _(u):
+        v, w = u // 2, lax.rem(u, 2)
+        far = (v + 1) // 2
+        dy = far + lax.rem(far, 2) * 2 * w
+        dc = v // 2 + (1 - (lax.rem(v, 3) + 1) // 2) * w * (1 - 2 * (v // 2))
+
+        @pl.when(u == 2)
+        def _():
+            half_copy(1, 0).wait_recv()
+            relay_copy(0).start()
+            half_copy(3, 1).wait_recv()
+            relay_copy(1).start()
+            half_copy(1, 1).wait_recv()
             forward_copy(1).start()
-            query_copy(3).wait_recv()
-            query_copy(2).start()
+            half_copy(3, 0).wait_recv()
             forward_copy(3).start()
 
-        @pl.when(t == 3)
-        def _():
-            query_copy(2).wait_recv()
+        @pl.when(u == 4)
+        def _():
+            relay_copy(0).wait_recv()
+            relay_copy(1).wait_recv()
             forward_copy(2).start()
 
-        part_own[dy] = to_lines(block_terms(from_lines(all_queries[dy, 0])))
-        forward_copy(dy).wait_recv()
-        part_other[dy] = to_lines(block_terms(from_lines(all_queries[dy, 1])))
-        sibling_copy(dy).start()
-
-        @pl.when(t > 1)
-        def _():
-            last = order(t - 1)
+        @pl.when(dc == 1)
+        def _():
+            forward_copy(dy).wait_recv()
+
+        parts[dy, dc] = to_lines(block_terms(from_lines(all_queries[dy, dc])))
+
+        @pl.when(dc == 1)
+        def _():
+            sibling_copy(dy).start()
+
+        @pl.when((u == 5) | (u == 6))
+        def _():
+            last = 1 + 2 * (u - 5)
             finish(last)
             home_copy(last).start()
 
@@ -579,8 +624,11 @@
         forward_copy(dy).wait_send()
         sibling_copy(dy).wait_send()
         if dy > 0:
-            query_copy(dy).wait_send()
             home_copy(dy).wait_send()
+    for half in range(2):
+        half_copy(1, half).wait_send()
+        half_copy(3, half).wait_send()
+        relay_copy(half).wait_send()
 
 
 def on_device(entity_table, adagrad_sum, relations, owner_map, head_ids, rel_ids, tail_ids, neg_ids):
@@ -590,7 +638,7 @@
     count = 2 * edges + neg_count
     map_rows = owner_map.shape[0] // 128
     vmem = pl.BlockSpec(memory_space=pltpu.VMEM)
-    hbm = pl.BlockSpec(memory_space=pl.ANY)
+    hbm = pl.BlockSpec(memory_space=pltpu.HBM)
     wide = 4 * LANES
     slots = pltpu.VMEM((DEVICES, LINES, LANES), F32)
     parts = pltpu.VMEM((4, width, LANES), F32)
@@ -601,9 +649,14 @@
             jax.ShapeDtypeStruct((width, rows_here), F32),
             jax.ShapeDtypeStruct((1, rows_here), F32),
         ),
-        in_specs=[vmem, vmem, vmem, vmem, hbm, hbm, hbm, vmem],
+        in_specs=[hbm] * 8,
         out_specs=(vmem, vmem),
         scratch_shapes=[
+            pltpu.VMEM((1, edges), jnp.int32),
+            pltpu.VMEM((1, edges), jnp.int32),
+            pltpu.VMEM((neg_count // LANES, LANES), jnp.int32),
+            pltpu.VMEM((1, edges), jnp.int32),
+            pltpu.VMEM((1, rows_here), F32),
             pltpu.VMEM((map_rows, 128), jnp.int32),
             pltpu.VMEM((width, rows_here), F32),
             pltpu.VMEM((width, -(-relations.shape[0] // (REL * REL_PARTS)) * REL), F32),
@@ -630,8 +683,7 @@
             pltpu.VMEM((neg_count, wide), F32),
             pltpu.VMEM((1, neg_count), F32),
             pltpu.VMEM((4, 2, width, LANES), F32),
-            parts,
-            parts,
+            pltpu.VMEM((4, 2, width, LANES), F32),
             parts,
             parts,
             parts,
@@ -639,28 +691,30 @@
             slots,
             slots,
             pltpu.VMEM((wide, rows_here), F32),
-            sem((3,)),
+            sem((8,)),
             sem((2,)),
             sem((CHUNKS,)),
             sem((CHUNKS,)),
             sem((4, 2)),
+            sem((4,)),
             sem((4, 2)),
             sem((4,)),
             sem((4, 2)),
+            sem((4,)),
             sem((4, 2)),
         ],
         compiler_params=pltpu.CompilerParams(
             collective_id=0, has_side_effects=True, vmem_limit_bytes=LIMIT
         ),
     )(
-        head_ids.reshape(1, edges),
-        tail_ids.reshape(1, edges),
-        neg_ids.reshape(neg_count // 128, 128),
-        rel_ids.reshape(1, edges),
-        owner_map.reshape(map_rows, 128),
-        entity_table.T,
-        relations.T,
-        adagrad_sum.reshape(1, rows_here),
+        pltpu.with_memory_space_constraint(head_ids.reshape(1, edges), pltpu.HBM),
+        pltpu.with_memory_space_constraint(tail_ids.reshape(1, edges), pltpu.HBM),
+        pltpu.with_memory_space_constraint(neg_ids.reshape(neg_count // 128, 128), pltpu.HBM),
+        pltpu.with_memory_space_constraint(rel_ids.reshape(1, edges), pltpu.HBM),
+        pltpu.with_memory_space_constraint(owner_map.reshape(map_rows, 128), pltpu.HBM),
+        pltpu.with_memory_space_constraint(entity_table.T, pltpu.HBM),
+        pltpu.with_memory_space_constraint(relations.T, pltpu.HBM),
+        pltpu.with_memory_space_constraint(adagrad_sum.reshape(1, rows_here), pltpu.HBM),
     )
     return new_table.T, new_sum.reshape(rows_here)
 

time: 129 us -> 124 us (0.961)
  local copies, waits for them, and re-layouts: 6.87 us -> 2.31 us
    unnamed x14 -> x2, local copies, waits for them, and re-layouts: 6.87 us -> 2.31 us
where the time goes in v4:
time: 124 us; the launch traced here: 122 us
  Pallas kernels  119 us (96%)
  local copies, waits for them, and re-layouts  2.31 us (2%)
    pallas_call x1, Pallas kernels, on_device(): pl.pallas_call(step_kernel, out_shape=(jax.ShapeDtypeStruct((width, rows_...  119 us

profile of v4, /device:TPU:1, one launch (start us, length us, event | category | flops | bytes accessed | tf_op | source)
XLA Modules:
  0.0 122.4 jit_solution(13760598970816339140)
XLA Ops:
  0.6 119.5 %shard_map.95 = (f32[400,2048]{1,0:T(8,128)S(1)}, f32[1,2048]{1,0:T(1,128)S(1)}) custom-call(s32[1,128]{1,0:T(1,128)} %bitcast.17, s32[1,128]{1,0:T(1,128)} %bitcast.18, s32[4,128]{1,0:T(4,128)} %bitcast.16, s32[1,128]{1,0:T(1,128)} %bitcast.19, s32[2048,128]{1,0:T(8,128)} %bitcast.14, f32[400,2048]{1,0:T(8,128)} %bitcast.13, f32[400,7424]{1,0:T(8,128)} %bitcast.12, ...), custom_call_target="tpu_custom_call" | custom-call | tf_op jit(solution)/shard_map/pallas_call | solution.py:646
  120.1 1.7 %copy.12 = f32[2048,400]{0,1:T(8,128)} copy(f32[2048,400]{0,1:T(8,128)S(1)} %bitcast.10) | data formatting | bytes 6553600
  121.8 0.6 copy.13

commit v5 on v4

--- a/solution.py
+++ b/solution.py
@@ -20,7 +20,7 @@
 CHUNKS = DEVICES // GROUP
 SLOTS = GROUP * PAD
 LINES = 40
-LIMIT = 48 * 1024 * 1024
+LIMIT = 50 * 1024 * 1024
 LANES = 128
 TAIL = 16
 REL = 256
@@ -488,17 +488,20 @@
             (dp, lax.rem(my + 4 - dy, 4) * 2 + mc),
         )
 
-    def block_terms(block):
+    def block_terms(block, where):
         pieces = split(block)
         block_sq = jnp.sum(block * block, axis=1, keepdims=True)
         neg_parts = (neg_pieces[0], neg_pieces[1])
-        inner = dot3(pieces, neg_parts, 1, 1)
+        both = dot(jnp.concatenate(pieces, axis=0), neg_parts[0], 1, 1)
+        inner = both[0:edges] + (both[edges:] + dot(pieces[0], neg_parts[1], 1, 1))
         dist = jnp.sqrt(block_sq + neg_sq - 2.0 * inner + EPSILON)
         coef = -1.0 / ((1.0 + jnp.exp(dist - MARGIN)) * (weight * dist))
         coef_parts = split(coef)
         coef_cols[...] += jnp.sum(coef, axis=0, keepdims=True)
         block_acc[...] += dot3(coef_parts, pieces, 0, 0)
-        return block * jnp.sum(coef, axis=1, keepdims=True) - dot3(coef_parts, neg_parts, 1, 0)
+        both = dot(jnp.concatenate(coef_parts, axis=0), neg_parts[0], 1, 0)
+        drawn = both[0:edges] + (both[edges:] + dot(coef_parts[0], neg_parts[1], 1, 0))
+        return block * jnp.sum(coef, axis=1, keepdims=True) - drawn
 
     def finish(dy):
         sibling_copy(dy).wait_recv()
@@ -532,7 +535,8 @@
         def _():
             forward_copy(dy).wait_recv()
 
-        parts[dy, dc] = to_lines(block_terms(from_lines(all_queries[dy, dc])))
+        where = pl.ds(pl.multiple_of(u * edges, edges), edges)
+        parts[dy, dc] = to_lines(block_terms(from_lines(all_queries[dy, dc]), where))
 
         @pl.when(dc == 1)
         def _():
@@ -547,25 +551,22 @@
     finish(2)
     home_copy(2).start()
     finish(0)
+    coef_col = jnp.concatenate(
+        [to_column(coef_cols[:, 128 * t : 128 * t + 128]) for t in range(neg_count // 128)], axis=0
+    )
+    spread = onehot(iota((LANES, LANES), 0) == lax.rem(iota((LANES, LANES), 1), TAIL))
+
+    def keep(first, last, value):
+        for n, piece in enumerate(split(value)):
+            grad_pieces[n, first:last, 0:body] = piece[:, 0:body]
+            grad_pieces[n, first:last, body:] = dot(piece[:, body:], spread, 1, 0).astype(BF16)
+
+    keep(edges, 2 * edges, -grad_pos)
+    keep(2 * edges, count, wanted[2 * edges :, :] * coef_col - block_acc[...])
     for dy in (1, 3, 2):
         home_copy(dy).wait_recv()
     grad_neg = from_lines((part_sum[0] + part_recv[1]) + (part_recv[2] + part_recv[3]))
-    high, low = split(grad_pos + grad_neg)
-    grad_pieces[0, 0:edges] = high
-    grad_pieces[1, 0:edges] = low
-    high, low = split(-grad_pos)
-    grad_pieces[0, edges : 2 * edges] = high
-    grad_pieces[1, edges : 2 * edges] = low
-    coef_col = jnp.concatenate(
-        [to_column(coef_cols[:, 128 * t : 128 * t + 128]) for t in range(neg_count // 128)], axis=0
-    )
-    high, low = split(wanted[2 * edges :, :] * coef_col - block_acc[...])
-    grad_pieces[0, 2 * edges :] = high
-    grad_pieces[1, 2 * edges :] = low
-
-    spread = onehot(iota((LANES, LANES), 0) == lax.rem(iota((LANES, LANES), 1), TAIL))
-    for n in range(2):
-        grad_pieces[n, :, body:] = dot(grad_pieces[n, :, body:], spread, 1, 0).astype(BF16)
+    keep(0, edges, grad_pos + grad_neg)
 
     def grad_copy(i):
         return remote(

time: 124 us -> 123 us (level)
  no operation moved by 1% of the time
where the time goes in v5:
time: 123 us; the launch traced here: 121 us
  Pallas kernels  118 us (96%)
  local copies, waits for them, and re-layouts  2.31 us (2%)
    pallas_call x1, Pallas kernels, on_device(): pl.pallas_call(step_kernel, out_shape=(jax.ShapeDtypeStruct((width, rows_...  118 us

profile of v5, /device:TPU:1, one launch (start us, length us, event | category | flops | bytes accessed | tf_op | source)
XLA Modules:
  0.0 121.4 jit_solution(10861904299915339796)
XLA Ops:
  0.6 118.5 %shard_map.95 = (f32[400,2048]{1,0:T(8,128)S(1)}, f32[1,2048]{1,0:T(1,128)S(1)}) custom-call(s32[1,128]{1,0:T(1,128)} %bitcast.17, s32[1,128]{1,0:T(1,128)} %bitcast.18, s32[4,128]{1,0:T(4,128)} %bitcast.16, s32[1,128]{1,0:T(1,128)} %bitcast.19, s32[2048,128]{1,0:T(8,128)} %bitcast.14, f32[400,2048]{1,0:T(8,128)} %bitcast.13, f32[400,7424]{1,0:T(8,128)} %bitcast.12, ...), custom_call_target="tpu_custom_call" | custom-call | tf_op jit(solution)/shard_map/pallas_call | solution.py:647
  119.1 1.7 %copy.12 = f32[2048,400]{0,1:T(8,128)} copy(f32[2048,400]{0,1:T(8,128)S(1)} %bitcast.10) | data formatting | bytes 6553600
  120.8 0.6 copy.13

commit v6 on v5

--- a/solution.py
+++ b/solution.py
@@ -307,6 +307,20 @@
     for t in range(6):
         slot_row[t : t + 1, :] = to_row(slot[128 * t : 128 * t + 128])
 
+    ask_mid[0] = ask_send[0]
+
+    pl.semaphore_wait(barrier, 22)
+
+    def group_ask(r):
+        return remote(ask_send.at[r], ask_mid.at[r], send_sems.at[0], ask_sems.at[0], in_group(r))
+
+    def plane_ask(p):
+        return remote(ask_sum.at[p], asked.at[p], send_sems.at[3], ask_sems.at[1], in_plane(p))
+
+    @pl.loop(1, 8)
+    def _(r):
+        group_ask(r).start()
+
     load_table.wait()
     high, low = split(table[...])
     table_high[0:width] = high
@@ -316,20 +330,6 @@
         table_low[body + TAIL * j : body + TAIL * j + TAIL] = low[body:]
     summed[...] = jnp.zeros_like(summed)
     wanted[...] = jnp.zeros_like(wanted)
-    ask_mid[0] = ask_send[0]
-
-    pl.semaphore_wait(barrier, 22)
-
-    def group_ask(r):
-        return remote(ask_send.at[r], ask_mid.at[r], send_sems.at[0], ask_sems.at[0], in_group(r))
-
-    def plane_ask(p):
-        return remote(ask_sum.at[p], asked.at[p], send_sems.at[3], ask_sems.at[1], in_plane(p))
-
-    @pl.loop(1, 8)
-    def _(r):
-        group_ask(r).start()
-
     part = ask_mid.at[pl.ds(1, 7)]
     pltpu.make_async_copy(part, part, ask_sems.at[0]).wait()
     ask_sum[...] = jnp.sum(ask_mid[...], axis=0)

time: 123 us -> 123 us (level)
  no operation moved by 1% of the time
where the time goes in v6:
time: 123 us; the launch traced here: 121 us
  Pallas kernels  118 us (96%)
  local copies, waits for them, and re-layouts  2.31 us (2%)
    pallas_call x1, Pallas kernels, on_device(): pl.pallas_call(step_kernel, out_shape=(jax.ShapeDtypeStruct((width, rows_...  118 us

profile of v6, /device:TPU:1, one launch (start us, length us, event | category | flops | bytes accessed | tf_op | source)
XLA Modules:
  0.0 120.6 jit_solution(1514274285113026216)
XLA Ops:
  0.6 117.7 %shard_map.95 = (f32[400,2048]{1,0:T(8,128)S(1)}, f32[1,2048]{1,0:T(1,128)S(1)}) custom-call(s32[1,128]{1,0:T(1,128)} %bitcast.17, s32[1,128]{1,0:T(1,128)} %bitcast.18, s32[4,128]{1,0:T(4,128)} %bitcast.16, s32[1,128]{1,0:T(1,128)} %bitcast.19, s32[2048,128]{1,0:T(8,128)} %bitcast.14, f32[400,2048]{1,0:T(8,128)} %bitcast.13, f32[400,7424]{1,0:T(8,128)} %bitcast.12, ...), custom_call_target="tpu_custom_call" | custom-call | tf_op jit(solution)/shard_map/pallas_call | solution.py:647
  118.3 1.7 %copy.12 = f32[2048,400]{0,1:T(8,128)} copy(f32[2048,400]{0,1:T(8,128)S(1)} %bitcast.10) | data formatting | bytes 6553600
  120.0 0.6 copy.13

commit v7 on v6

--- a/solution.py
+++ b/solution.py
@@ -212,6 +212,22 @@
             device_id_type=MESH,
         )
 
+    barrier = pltpu.get_barrier_semaphore()
+
+    def in_group(r):
+        return dp, lax.rem(my + lax.rem(r, 4), 4) * 2 + lax.rem(mc + r // 4, 2)
+
+    def in_plane(p):
+        return lax.rem(mx + p // 4, 4) * 4 + lax.rem(mz + lax.rem(p, 4), 4), blk
+
+    @pl.loop(1, 8)
+    def _(r):
+        pl.semaphore_signal(barrier, inc=1, device_id=in_group(r), device_id_type=MESH)
+
+    @pl.loop(1, 16)
+    def _(p):
+        pl.semaphore_signal(barrier, inc=1, device_id=in_plane(p), device_id_type=MESH)
+
     load_map = pltpu.make_async_copy(map_hbm, map_ref, load_sem.at[0])
     load_table = pltpu.make_async_copy(table_hbm, table, load_sem.at[1])
 
@@ -237,22 +253,6 @@
     load_map.start()
     load_table.start()
     load_relations(0).start()
-    barrier = pltpu.get_barrier_semaphore()
-
-    def in_group(r):
-        return dp, lax.rem(my + lax.rem(r, 4), 4) * 2 + lax.rem(mc + r // 4, 2)
-
-    def in_plane(p):
-        return lax.rem(mx + p // 4, 4) * 4 + lax.rem(mz + lax.rem(p, 4), 4), blk
-
-    @pl.loop(1, 8)
-    def _(r):
-        pl.semaphore_signal(barrier, inc=1, device_id=in_group(r), device_id_type=MESH)
-
-    @pl.loop(1, 16)
-    def _(p):
-        pl.semaphore_signal(barrier, inc=1, device_id=in_plane(p), device_id_type=MESH)
-
     for copy in small:
         copy.wait()
     ids[0:1, :] = heads[...]
@@ -302,11 +302,6 @@
     lower = jnp.where(spot, (local & 255).astype(F32), 0.0).astype(BF16)
     asks = 256.0 * dot(key_hot, upper, 0, 0) + dot(key_hot, lower, 0, 0)
     ask_send[...] = asks.reshape(8, 16, 1, LANES)
-    slot = keys * float(PAD) + rank
-    slot_col[...] = slot
-    for t in range(6):
-        slot_row[t : t + 1, :] = to_row(slot[128 * t : 128 * t + 128])
-
     ask_mid[0] = ask_send[0]
 
     pl.semaphore_wait(barrier, 22)
@@ -330,6 +325,11 @@
         table_low[body + TAIL * j : body + TAIL * j + TAIL] = low[body:]
     summed[...] = jnp.zeros_like(summed)
     wanted[...] = jnp.zeros_like(wanted)
+    slot = keys * float(PAD) + rank
+    slot_col[...] = slot
+    for t in range(6):
+        slot_row[t : t + 1, :] = to_row(slot[128 * t : 128 * t + 128])
+
     part = ask_mid.at[pl.ds(1, 7)]
     pltpu.make_async_copy(part, part, ask_sems.at[0]).wait()
     ask_sum[...] = jnp.sum(ask_mid[...], axis=0)

time: 123 us -> 123 us (level)
  no operation moved by 1% of the time
where the time goes in v7:
time: 123 us; the launch traced here: 121 us
  Pallas kernels  118 us (96%)
  local copies, waits for them, and re-layouts  2.31 us (2%)
    pallas_call x1, Pallas kernels, on_device(): pl.pallas_call(step_kernel, out_shape=(jax.ShapeDtypeStruct((width, rows_...  118 us

profile of v7, /device:TPU:1, one launch (start us, length us, event | category | flops | bytes accessed | tf_op | source)
XLA Modules:
  0.0 121.1 jit_solution(5469554966033773503)
XLA Ops:
  0.6 118.1 %shard_map.95 = (f32[400,2048]{1,0:T(8,128)S(1)}, f32[1,2048]{1,0:T(1,128)S(1)}) custom-call(s32[1,128]{1,0:T(1,128)} %bitcast.17, s32[1,128]{1,0:T(1,128)} %bitcast.18, s32[4,128]{1,0:T(4,128)} %bitcast.16, s32[1,128]{1,0:T(1,128)} %bitcast.19, s32[2048,128]{1,0:T(8,128)} %bitcast.14, f32[400,2048]{1,0:T(8,128)} %bitcast.13, f32[400,7424]{1,0:T(8,128)} %bitcast.12, ...), custom_call_target="tpu_custom_call" | custom-call | tf_op jit(solution)/shard_map/pallas_call | solution.py:647
  118.8 1.7 %copy.12 = f32[2048,400]{0,1:T(8,128)} copy(f32[2048,400]{0,1:T(8,128)S(1)} %bitcast.10) | data formatting | bytes 6553600
  120.5 0.6 copy.13
